TPU v7x, 128 devices: a whole 4x4x4 slice. The times are simulated.
128 devices in a mesh: req: 16 (over y, z), mlp: 8 (over x, core).
Axes of the slice: x: 4, y: 4, z: 4, core: 2. Of those that a mesh axis runs over, the one named last changes fastest.
Arguments:
- queries: bfloat16 [2048, 5120], P('req', 'mlp'), may hold values from -6 to 6
- leaf_keys: bfloat16 [2048, 1024], P('req', 'mlp'), may hold values from -6 to 6
- leaf_token_values: bfloat16 [2048, 1024], P('req', 'mlp'), may hold values from -6 to 6
- key_value_pages: bfloat16 [512, 64, 2, 1024], P('req', None, None, 'mlp'), may hold values from -6 to 6
- page_holder: int32 [16, 6, 4], replicated, may hold values from 0 to 15, as said below
- page_slot: int32 [16, 6, 4], replicated, may hold values from 0 to 31
- segment_ids: int32 [2048], P('req'), may hold values from 0 to 7, as said below
- req_parent: int32 [16, 8], P('req'), may hold values from 0 to 3
- mid_parent: int32 [16, 4], P('req'), may hold values from 0 to 1
- node_len: int32 [16, 6], P('req'), may hold values from 1 to 256
- residual: bfloat16 [2048, 5120], P('req'), may hold values from -6 to 6
- out_proj: bfloat16 [5120, 5120], P('mlp'), may hold values from -0.078125 to 0.078125
- norm_gain: float32 [5120], replicated, may hold values from 0.5 to 1.5
- gate_proj: bfloat16 [5120, 13824], P(None, ('req', 'mlp')), may hold values from -0.078125 to 0.078125
- up_proj: bfloat16 [5120, 13824], P(None, ('req', 'mlp')), may hold values from -0.078125 to 0.078125
- down_proj: bfloat16 [13824, 5120], P(('req', 'mlp')), may hold values from -0.0546875 to 0.0546875
- next_gain: float32 [5120], replicated, may hold values from 0.5 to 1.5
- qkv_proj: bfloat16 [5120, 7168], P(None, 'mlp'), may hold values from -0.078125 to 0.078125
- qkv_bias: float32 [7168], P('mlp'), may hold values from -3 to 3
Outputs:
- layer_out: bfloat16 [2048, 5120], P(('req', 'mlp'))
- qkv_out: bfloat16 [2048, 7168], P('req', 'mlp')
Inputs may be any that keep to these rules, and one draw needn't show every extreme that they name: `segment_ids`: within each block of 128 tokens of one group the ids never fall, start at 0, and every id 0 to 7 occurs. `page_holder`: in each row (one group's prefix pages) exactly half of the entries name the row's own group; the other entries name other groups, no group more than 1 times in a row, and some group exactly 1 times.
All inputs are finite; a program needn't handle non-finite values.
Results may differ from a plain program's by a relative error of at most 0.02.
Values may be sent and summed in bfloat16 or wider, within the bound.
A program may use at most 192 MiB of HBM per device.

v0:
```python
import math

import jax
import jax.numpy as jnp
from jax import lax
from jax.sharding import PartitionSpec as P

HEAD_SIZE = 128
QUERY_PER_KV = 5
REQ_DEV = 8
ROOT_DEV = 2
MID_DEV = 4
NODES_DEV = 6
NODE_MAX = 256


EPS = 1e-06


def rms_norm(stream, gain):
    values = stream.astype(jnp.float32)
    mean_sq = jnp.mean(values * values, axis=-1, keepdims=True)
    return (values * lax.rsqrt(mean_sq + EPS) * gain).astype(jnp.bfloat16)


def attend(
    queries,
    leaf_keys,
    leaf_token_values,
    prefix_keys,
    prefix_values,
    segments,
    parents,
    roots,
    lengths,
):
    tokens = queries.shape[0]
    heads_kv = leaf_keys.shape[1] // HEAD_SIZE
    query_rows = queries.reshape(tokens, heads_kv, QUERY_PER_KV, HEAD_SIZE)
    keys = jnp.concatenate(
        [
            prefix_keys.reshape(-1, heads_kv, HEAD_SIZE),
            leaf_keys.reshape(tokens, heads_kv, HEAD_SIZE),
        ],
        0,
    )
    values = jnp.concatenate(
        [
            prefix_values.reshape(-1, heads_kv, HEAD_SIZE),
            leaf_token_values.reshape(tokens, heads_kv, HEAD_SIZE),
        ],
        0,
    )
    middle = jnp.sum((segments[:, None] == jnp.arange(REQ_DEV)[None, :]) * parents[None, :], axis=1)
    root = jnp.sum((middle[:, None] == jnp.arange(MID_DEV)[None, :]) * roots[None, :], axis=1)
    node = jnp.arange(NODES_DEV * NODE_MAX) // NODE_MAX
    inside = (jnp.arange(NODE_MAX)[None, :] < lengths[:, None]).reshape(-1)
    prefix_mask = (
        (node[None, :] == root[:, None]) | (node[None, :] == ROOT_DEV + middle[:, None])
    ) & inside[None, :]
    place = jnp.arange(tokens)
    leaf_mask = (segments[None, :] == segments[:, None]) & (place[None, :] <= place[:, None])
    mask = jnp.concatenate([prefix_mask, leaf_mask], 1)
    score = jnp.einsum(
        "tkgd,skd->tkgs", query_rows, keys, preferred_element_type=jnp.float32
    ) / math.sqrt(HEAD_SIZE)
    score = jnp.where(mask[:, None, None, :], score, -1e30)
    top = jnp.max(score, axis=-1, keepdims=True)
    expo = jnp.where(mask[:, None, None, :], jnp.exp(score - top), 0.0)
    total = jnp.sum(expo, axis=-1, keepdims=True)
    weights = expo.astype(jnp.bfloat16)
    summed = jnp.einsum("tkgs,skd->tkgd", weights, values, preferred_element_type=jnp.float32)
    return (summed / total).astype(jnp.bfloat16).reshape(tokens, -1)


def fetch_prefix(key_value_pages, page_holder, page_slot):
    groups = lax.axis_size("req")
    myself = lax.axis_index("req")
    holders = page_holder.reshape(groups, -1)
    slots = page_slot.reshape(groups, -1)
    token_count = holders.shape[1]
    room = (token_count // 2 + groups - 2) // (groups - 1)
    earlier = jnp.arange(token_count)[None, :] < jnp.arange(token_count)[:, None]
    same = holders[:, :, None] == holders[:, None, :]
    rank = jnp.sum(same & earlier[None, :, :], axis=-1)
    asked = (holders == myself) & (jnp.arange(groups)[:, None] != myself)
    picked = asked[:, None, :] & (rank[:, None, :] == jnp.arange(room)[None, :, None])
    send_slot = jnp.sum(jnp.where(picked, slots[:, None, :], 0), axis=-1)
    outgoing = key_value_pages[send_slot]
    incoming = lax.all_to_all(outgoing, "req", split_axis=0, concat_axis=0, tiled=True)
    flat_in = incoming.reshape((groups * room,) + incoming.shape[2:])
    own_holders = lax.dynamic_index_in_dim(holders, myself, 0, keepdims=False)
    own_slots = lax.dynamic_index_in_dim(slots, myself, 0, keepdims=False)
    own_rank = lax.dynamic_index_in_dim(rank, myself, 0, keepdims=False)
    remote = flat_in[own_holders * room + jnp.minimum(own_rank, room - 1)]
    local = key_value_pages[own_slots]
    pages = jnp.where((own_holders == myself)[:, None, None, None], local, remote)
    return pages.reshape(NODES_DEV * NODE_MAX, 2, -1)


def body(
    queries,
    leaf_keys,
    leaf_token_values,
    key_value_pages,
    page_holder,
    page_slot,
    segment_ids,
    req_parent,
    mid_parent,
    node_len,
    residual,
    out_proj,
    norm_gain,
    gate_proj,
    up_proj,
    down_proj,
    next_gain,
    qkv_proj,
    qkv_bias,
):
    prefix = fetch_prefix(key_value_pages, page_holder, page_slot)
    attention = attend(
        queries,
        leaf_keys,
        leaf_token_values,
        prefix[:, 0],
        prefix[:, 1],
        segment_ids,
        req_parent[0],
        mid_parent[0],
        node_len[0],
    )
    projected = jnp.dot(attention, out_proj, preferred_element_type=jnp.float32)
    group_tokens = queries.shape[0]
    groups = lax.axis_size("req")
    members = lax.axis_size("mlp")
    rows_mlp = group_tokens // members
    first_row = lax.axis_index("mlp") * rows_mlp
    head_part = lax.psum_scatter(
        projected.astype(jnp.bfloat16), "mlp", scatter_dimension=0, tiled=True
    ).astype(jnp.float32)
    own_resid = lax.dynamic_slice_in_dim(residual, first_row, rows_mlp, 0)
    stream = (own_resid.astype(jnp.float32) + head_part).astype(jnp.bfloat16)
    normed = rms_norm(stream, norm_gain)
    piece = lax.all_gather(normed, ("req", "mlp"), axis=0, tiled=True)
    gate = jnp.dot(piece, gate_proj, preferred_element_type=jnp.float32)
    upper = jnp.dot(piece, up_proj, preferred_element_type=jnp.float32)
    hidden_all = (jax.nn.silu(gate) * upper).astype(jnp.bfloat16)
    blocks = hidden_all.reshape(groups, members, rows_mlp, -1)
    regrouped = lax.all_to_all(blocks, "mlp", split_axis=1, concat_axis=3, tiled=True)
    hidden = regrouped.reshape(groups * rows_mlp, -1)
    mixed_all = jnp.dot(
        hidden,
        lax.all_gather(down_proj, "mlp", axis=0, tiled=True),
        preferred_element_type=jnp.float32,
    )
    mixed = lax.psum_scatter(
        mixed_all.astype(jnp.bfloat16), "req", scatter_dimension=0, tiled=True
    ).astype(jnp.float32)
    layer_out = (stream.astype(jnp.float32) + mixed).astype(jnp.bfloat16)
    next_rows = rms_norm(layer_out, next_gain)
    next_normed = lax.all_gather(next_rows, "mlp", axis=0, tiled=True)
    qkv_out = (
        jnp.dot(next_normed, qkv_proj, preferred_element_type=jnp.float32) + qkv_bias
    ).astype(jnp.bfloat16)
    return (layer_out, qkv_out)


def solution(mesh):
    placed = (
        P("req", "mlp"),
        P("req", "mlp"),
        P("req", "mlp"),
        P("req", None, None, "mlp"),
        P(),
        P(),
        P("req"),
        P("req", None),
        P("req", None),
        P("req", None),
        P("req", None),
        P("mlp", None),
        P(),
        P(None, ("req", "mlp")),
        P(None, ("req", "mlp")),
        P(("req", "mlp"), None),
        P(),
        P(None, "mlp"),
        P("mlp"),
    )
    return jax.shard_map(
        body,
        mesh=mesh,
        in_specs=placed,
        out_specs=(P(("req", "mlp"), None), P("req", "mlp")),
        check_vma=False,
    )
```

profile of v0, /device:TPU:1, one launch (start us, length us, event | category | flops | bytes accessed | tf_op | source)
XLA Modules:
  0.0 356.3 jit_solution(15968638742785638937)
XLA Ops:
  7.2 0.0 copy-start
  7.2 0.9 copy.70
  8.1 0.4 convert_reduce_fusion
  8.6 0.1 copy.75
  8.7 0.8 select_reduce_fusion
  9.5 3.6 %gather_fusion.1 = bf16[16,64,2,128]{3,2,1,0:T(2,128)(2,1)} fusion(bf16[32,64,2,128]{3,2,1,0:T(2,128)(2,1)} %param.22, s32[1024]{0:T(1024)S(1)} %pad_clamp_fusion.1), kind=kCustom, calls=%fused_computation.1 | custom fusion | bytes 1048640 | tf_op jit(solution)/shard_map/gather | solution.py:89
  13.1 8.6 %all-to-all-start = ((bf16[16,1,64,2,128]{4,3,2,1,0:T(2,128)(2,1)}), bf16[16,1,64,2,128]{4,3,2,1,0:T(2,128)(2,1)S(1)}, u32[]{:S(2)}, u32[]{:S(2)}) async-start(bf16[16,1,64,2,128]{4,3,2,1,0:T(2,128)(2,1)} %bitcast.9), calls=%async_computation | async-start | bytes 1048576 | tf_op jit(solution)/shard_map/all_to_all | solution.py:90
  21.7 0.0 reduce-scatter.3.cloned.1.call-start
  21.8 0.8 constant_dynamic-slice_fusion.1
  22.5 0.1 copy.88
  22.6 0.8 select_reduce_fusion.1
  23.4 0.7 select_reduce_fusion.2
  24.2 0.7 iota_compare_fusion.2
  24.9 1.7 or_and_fusion
  26.6 0.1 broadcast_in_dim.28
  26.7 0.1 broadcast_in_dim.29
  26.8 3.4 gather_fusion
  30.1 0.2 copy.72
  30.4 0.0 copy-start.11
  30.4 0.8 copy.77
  31.2 0.1 fusion.30
  31.3 0.9 pad_add_fusion
  32.2 2.1 gather_fusion.2
  34.4 0.0 copy-start.4
  34.4 0.2 copy.76
  34.6 0.3 bitcast_select_fusion.1
  34.9 0.1 fusion.45
  35.0 0.3 copy-done.4
  35.3 0.8 fusion
  36.1 0.0 slice-start
  36.1 1.0 fusion.1
  37.1 0.0 slice-start.1
  37.2 1.3 fusion.15
  38.4 1.0 slice-done.1
  39.5 2.3 convolution_convert_fusion.1
  41.8 0.0 reduce-scatter.3.cloned.1.call-update
  41.9 0.0 all-gather.5.cloned.1.call-start
  41.9 31.3 %reduce-scatter.3.cloned.1.call-done = bf16[16,5120]{1,0:T(8,128)(2,1)} async-done(((bf16[128,5120]{1,0:T(8,128)(2,1)}), bf16[16,5120]{1,0:T(8,128)(2,1)}) %reduce-scatter.3.cloned.1.call-update) | async-done | bytes 163856 | tf_op jit(solution)/shard_map/reduce_scatter | solution.py:140
  73.2 1.2 fusion.26
  74.4 0.8 fusion.28
  75.2 0.0 all-gather.5.cloned.1.call-update
  75.2 0.2 all-gather.9.cloned.1.call-start
  75.4 0.5 all-gather.9.cloned.1.call-update
  75.9 0.0 copy-start.10
  75.9 90.1 %all-gather.5.cloned.1.call-done = bf16[2048,5120]{1,0:T(8,128)(2,1)} async-done(((bf16[16,5120]{1,0:T(8,128)(2,1)}), bf16[2048,5120]{1,0:T(8,128)(2,1)}) %all-gather.5.cloned.1.call-update) | async-done | bytes 20971536 | tf_op jit(solution)/shard_map/all_gather | solution.py:146
  166.1 13.8 %fusion.46 = f32[2048,108]{0,1:T(8,128)S(1)} fusion(bf16[2048,5120]{1,0:T(8,128)(2,1)} %all-gather.5.cloned.1.call-done, bf16[5120,108]{0,1:T(8,128)(2,1)S(1)} %copy-done), kind=kOutput, calls=%fused_computation.86 | convolution fusion | flops 2264924160 | bytes 22962176 | tf_op jit(solution)/shard_map/dot_general | solution.py:147
  179.9 0.6 copy-done.9
  180.5 6.8 %fusion.3 = bf16[2048,108]{0,1:T(8,128)(2,1)S(1)} fusion(bf16[2048,5120]{1,0:T(8,128)(2,1)S(1)} %copy-done.9, bf16[5120,108]{0,1:T(8,128)(2,1)S(1)} %copy-done.10, f32[2048,108]{0,1:T(8,128)S(1)} %fusion.46), kind=kOutput, calls=%fused_computation.11 | convolution fusion | flops 2266251264 | bytes 23404544 | tf_op jit(solution)/shard_map/dot_general | solution.py:148
  187.3 0.3 copy.81
  187.5 0.9 copy.82
  188.4 4.3 %all-to-all-start.1 = ((bf16[16,8,16,108]{3,2,0,1:T(8,128)(2,1)}), bf16[16,8,16,108]{3,2,0,1:T(8,128)(2,1)S(1)}, u32[]{:S(2)}, u32[]{:S(2)}) async-start(bf16[16,8,16,108]{3,2,0,1:T(8,128)(2,1)} %copy.82), calls=%async_computation.2 | async-start | bytes 1048576 | tf_op jit(solution)/shard_map/all_to_all | solution.py:151
  192.7 33.1 %all-gather.9.cloned.1.call-done = bf16[8,108,5120]{2,1,0:T(8,128)(2,1)} async-done(((bf16[1,108,5120]{2,1,0:T(8,128)(2,1)}), bf16[8,108,5120]{2,1,0:T(8,128)(2,1)}) %all-gather.9.cloned.1.call-update) | async-done | bytes 8847376 | tf_op jit(solution)/shard_map/all_gather | solution.py:155
  225.8 8.0 %reshape.279 = bf16[864,5120]{1,0:T(8,128)(2,1)} reshape(bf16[8,108,5120]{2,1,0:T(8,128)(2,1)} %all-gather.9.cloned.1.call-done) | data formatting | bytes 17694720
  233.8 0.3 copy.83
  234.1 0.4 reshape.253
  234.6 7.7 %convolution_convert_fusion = bf16[256,5120]{1,0:T(8,128)(2,1)} fusion(bf16[256,864]{1,0:T(8,128)(2,1)S(1)} %reshape.253, bf16[864,5120]{1,0:T(8,128)(2,1)} %reshape.279), kind=kOutput, calls=%fused_computation.3 | convolution fusion | flops 2266234880 | bytes 11911168 | tf_op jit(solution)/shard_map/dot_general | solution.py:153
  242.3 0.0 reduce-scatter.5.cloned.1.call-update
  242.3 0.0 all-gather.7.cloned.1.call-start
  242.3 73.7 %reduce-scatter.5.cloned.1.call-done = bf16[16,5120]{1,0:T(8,128)(2,1)} async-done(((bf16[256,5120]{1,0:T(8,128)(2,1)}), bf16[16,5120]{1,0:T(8,128)(2,1)}) %reduce-scatter.5.cloned.1.call-update) | async-done | bytes 163856 | tf_op jit(solution)/shard_map/reduce_scatter | solution.py:158
  316.1 1.1 fusion.23
  317.2 0.8 fusion.25
  317.9 0.0 all-gather.7.cloned.1.call-update
  318.0 25.4 %all-gather.7.cloned.1.call-done = bf16[128,5120]{1,0:T(8,128)(2,1)} async-done(((bf16[16,5120]{1,0:T(8,128)(2,1)}), bf16[128,5120]{1,0:T(8,128)(2,1)}) %all-gather.7.cloned.1.call-update) | async-done | bytes 1310736 | tf_op jit(solution)/shard_map/all_gather | solution.py:163
  343.4 6.3 %fusion.8 = bf16[128,896]{1,0:T(8,128)(2,1)} fusion(bf16[128,5120]{1,0:T(8,128)(2,1)} %all-gather.7.cloned.1.call-done, bf16[5120,896]{1,0:T(8,128)(2,1)} %param.36, f32[896]{0:T(1024)S(1)} %copy-done.7), kind=kOutput, calls=%fused_computation.16 | convolution fusion | flops 1174634496 | bytes 10718720 | tf_op jit(solution)/shard_map/dot_general | solution.py:165
  (40 shorter events, 0.2 us)
Async XLA Ops:
  7.2 158.9 %copy-start = (bf16[5120,108]{0,1:T(8,128)(2,1)S(1)}, bf16[5120,108]{0,1:T(8,128)(2,1)}, u32[]{:S(2)}) copy-start(bf16[5120,108]{0,1:T(8,128)(2,1)} %param.32) | copy-start | bytes 3317764
  7.2 24.0 %copy-start.8 = (s32[128]{0:T(128)S(1)}, s32[128]{0:T(128)}, u32[]{:S(2)}) copy-start(s32[128]{0:T(128)} %param.25) | copy-start | bytes 1540
  7.2 23.2 %copy-start.3 = (bf16[128,640]{1,0:T(8,128)(2,1)S(1)}, bf16[128,640]{1,0:T(8,128)(2,1)}, u32[]{:S(2)}) copy-start(bf16[128,640]{1,0:T(8,128)(2,1)} %param.19) | copy-start | bytes 491524
  13.1 19.2 %all-to-all-start = ((bf16[16,1,64,2,128]{4,3,2,1,0:T(2,128)(2,1)}), bf16[16,1,64,2,128]{4,3,2,1,0:T(2,128)(2,1)S(1)}, u32[]{:S(2)}, u32[]{:S(2)}) async-start(bf16[16,1,64,2,128]{4,3,2,1,0:T(2,128)(2,1)} %bitcast.9), calls=%async_computation | async-start | bytes 1048576 | tf_op jit(solution)/shard_map/all_to_all | solution.py:90
  21.7 51.5 %reduce-scatter.3.cloned.1.call-start = ((), (), s32[]{:S(2)}) async-start(), calls=%async_computation.4 | async-start | bytes 1474560 | tf_op jit(solution)/shard_map/reduce_scatter | solution.py:140
  30.4 4.6 %copy-start.11 = (bf16[128,128]{1,0:T(8,128)(2,1)S(1)}, bf16[128,128]{1,0:T(8,128)(2,1)}, u32[]{:S(2)}) copy-start(bf16[128,128]{1,0:T(8,128)(2,1)} %param.20) | copy-start | bytes 98308
  34.4 0.9 copy-start.4
  35.3 1.9 copy-start.12
  36.1 2.4 slice-start
  37.1 2.3 slice-start.1
  39.5 34.9 %copy-start.5 = (f32[5120]{0:T(1024)S(1)}, f32[5120]{0:T(1024)}, u32[]{:S(2)}) copy-start(f32[5120]{0:T(1024)} %param.31) | copy-start | bytes 61444
  41.9 124.2 %all-gather.5.cloned.1.call-start = ((), (), s32[]{:S(2)}) async-start(), calls=%async_computation.5 | async-start | bytes 21135360 | tf_op jit(solution)/shard_map/all_gather | solution.py:146
  75.2 150.6 %all-gather.9.cloned.1.call-start = ((), (), s32[]{:S(2)}) async-start(), calls=%async_computation.8 | async-start | bytes 10321920 | tf_op jit(solution)/shard_map/all_gather | solution.py:155
  75.9 104.0 %copy-start.10 = (bf16[5120,108]{0,1:T(8,128)(2,1)S(1)}, bf16[5120,108]{0,1:T(8,128)(2,1)}, u32[]{:S(2)}) copy-start(bf16[5120,108]{0,1:T(8,128)(2,1)} %param.33) | copy-start | bytes 3317764
  166.1 14.4 %copy-start.9 = (bf16[2048,5120]{1,0:T(8,128)(2,1)S(1)}, bf16[2048,5120]{1,0:T(8,128)(2,1)}, u32[]{:S(2)}) copy-start(bf16[2048,5120]{1,0:T(8,128)(2,1)} %all-gather.5.cloned.1.call-done) | copy-start | bytes 62914564
  188.4 45.4 %all-to-all-start.1 = ((bf16[16,8,16,108]{3,2,0,1:T(8,128)(2,1)}), bf16[16,8,16,108]{3,2,0,1:T(8,128)(2,1)S(1)}, u32[]{:S(2)}, u32[]{:S(2)}) async-start(bf16[16,8,16,108]{3,2,0,1:T(8,128)(2,1)} %copy.82), calls=%async_computation.2 | async-start | bytes 1048576 | tf_op jit(solution)/shard_map/all_to_all | solution.py:151
  192.7 123.4 %reduce-scatter.5.cloned.1.call-start = ((), (), s32[]{:S(2)}) async-start(), calls=%async_computation.6 | async-start | bytes 2785280 | tf_op jit(solution)/shard_map/reduce_scatter | solution.py:158
  234.6 82.6 %copy-start.6 = (f32[5120]{0:T(1024)S(1)}, f32[5120]{0:T(1024)}, u32[]{:S(2)}) copy-start(f32[5120]{0:T(1024)} %param.35) | copy-start | bytes 61444
  234.6 108.8 %copy-start.7 = (f32[896]{0:T(1024)S(1)}, f32[896]{0:T(1024)}, u32[]{:S(2)}) copy-start(f32[896]{0:T(1024)} %param.37) | copy-start | bytes 10756
  242.3 101.1 %all-gather.7.cloned.1.call-start = ((), (), s32[]{:S(2)}) async-start(), calls=%async_computation.7 | async-start | bytes 1474560 | tf_op jit(solution)/shard_map/all_gather | solution.py:163
  317.1 32.6 %copy-start.2 = (bf16[16,5120]{1,0:T(8,128)(2,1)}, bf16[16,5120]{1,0:T(8,128)(2,1)S(1)}, u32[]{:S(2)}) copy-start(bf16[16,5120]{1,0:T(8,128)(2,1)S(1)} %get-tuple-element.3) | copy-start | bytes 491524
  343.4 6.3 %copy-start.1 = (bf16[5120,108]{0,1:T(8,128)(2,1)S(1)}, bf16[5120,108]{0,1:T(8,128)(2,1)}, u32[]{:S(2)}) copy-start(bf16[5120,108]{0,1:T(8,128)(2,1)} %param.32) | copy-start | bytes 3317764
Sparse Core Ops, SparseCore 0:
  42.0 31.1 reduce-scatter.2
  76.8 89.2 all-gather.4
  167.8 58.0 all-gather.8
  242.4 73.6 reduce-scatter.4
  318.2 25.1 all-gather.6
where the time goes:
time: 357 us; the launch traced here: 356 us
  waiting for transfers between devices  254 us (71%)
  matrix products  39 us (11%)
  local copies, waits for them, and re-layouts  24.3 us (7%)
  between operations  14.1 us (4%)
  starting transfers between devices  13.2 us (4%)
  other arithmetic  11.4 us (3%)
    all_gather x1, waiting for transfers between devices, body(): piece = lax.all_gather(normed, ('req', 'mlp'), axis=0, tiled=True)  90.1 us
    reduce_scatter x1, waiting for transfers between devices, body(): lax.psum_scatter(mixed_all.astype(jnp.bfloat16), 'req', scatter_dimension...  73.7 us
    all_gather x1, waiting for transfers between devices, body(): lax.all_gather(down_proj, 'mlp', axis=0, tiled=True)  33.1 us
    reduce_scatter x1, waiting for transfers between devices, body(): lax.psum_scatter(projected.astype(jnp.bfloat16), 'mlp', scatter_dimension...  31.3 us
    all_gather x1, waiting for transfers between devices, body(): next_normed = lax.all_gather(next_rows, 'mlp', axis=0, tiled=True)  25.4 us
    dot_general x1, matrix products, body(): gate = jnp.dot(piece, gate_proj, preferred_element_type=jnp.float32)  13.8 us
    unnamed x33, local copies, waits for them, and re-layouts  10.9 us
    all_to_all x1, starting transfers between devices, fetch_prefix(): lax.all_to_all(outgoing, 'req', split_axis=0, concat_axis=0, tiled=True)  8.6 us
  transfers between devices with their start and end apart: 7, of which 5 were waited for; matrix products, arithmetic and copies ran while one was open for 11% of the time, Pallas kernels for 0%

commit v1 on v0

--- a/solution.py
+++ b/solution.py
@@ -1,8 +1,11 @@
+import functools
 import math
 
 import jax
 import jax.numpy as jnp
 from jax import lax
+from jax.experimental import pallas as pl
+from jax.experimental.pallas import tpu as pltpu
 from jax.sharding import PartitionSpec as P
 
 HEAD_SIZE = 128
@@ -12,15 +15,16 @@
 MID_DEV = 4
 NODES_DEV = 6
 NODE_MAX = 256
-
+MODEL = 5120
+ROWS = 16
+UNITS = 108
+UNITS_PAD = 128
+DOWN_PAD = 112
+QKV_COLS = 896
 
 EPS = 1e-06
 
-
-def rms_norm(stream, gain):
-    values = stream.astype(jnp.float32)
-    mean_sq = jnp.mean(values * values, axis=-1, keepdims=True)
-    return (values * lax.rsqrt(mean_sq + EPS) * gain).astype(jnp.bfloat16)
+MESH = pl.DeviceIdType.MESH
 
 
 def attend(
@@ -98,6 +102,432 @@
     return pages.reshape(NODES_DEV * NODE_MAX, 2, -1)
 
 
+def place():
+    req = lax.axis_index("req")
+    mlp = lax.axis_index("mlp")
+    return lax.div(mlp, 2), lax.div(req, 4), lax.rem(req, 4), lax.rem(mlp, 2)
+
+
+def device(x, y, z, core):
+    return (y * 4 + z, x * 2 + core)
+
+
+def ahead(coords, axis, steps):
+    moved = list(coords)
+    moved[axis] = lax.rem(moved[axis] + steps, 4)
+    return moved
+
+
+def greet(x, y, z, core):
+    barrier = pltpu.get_barrier_semaphore()
+    others = [device(x, y, z, 1 - core)]
+    for axis in range(3):
+        for steps in (1, 2, 3):
+            others.append(device(*ahead((x, y, z), axis, steps), core))
+    for other in others:
+        pl.semaphore_signal(barrier, inc=1, device_id=other, device_id_type=MESH)
+    pl.semaphore_wait(barrier, len(others))
+
+
+def remote(src, dst, send, recv, target):
+    return pltpu.make_async_remote_copy(
+        src_ref=src, dst_ref=dst, send_sem=send, recv_sem=recv, device_id=target, device_id_type=MESH
+    )
+
+
+def normed_rows(rows, gain):
+    mean_sq = jnp.mean(rows * rows, axis=-1, keepdims=True)
+    return (rows * lax.rsqrt(mean_sq + EPS) * gain).astype(jnp.bfloat16)
+
+
+PARTS = (
+    (0, 1664, (1, 2, 0)),
+    (1664, 1664, (2, 0, 1)),
+    (3328, 1792, (0, 1, 2)),
+)
+
+
+def spread_kernel(
+    projected,
+    residual,
+    gain,
+    weights_hbm,
+    stream_out,
+    hidden_out,
+    resid,
+    half,
+    summed,
+    arrived,
+    tokens,
+    weights,
+    hidden,
+    local_sem,
+    half_send,
+    half_recv,
+    sum_send,
+    sum_recv,
+    weight_sem,
+    part_send,
+    part_recv,
+    hid_send,
+    hid_recv,
+):
+    x, y, z, core = place()
+    here = (x, y, z)
+    sibling = device(x, y, z, 1 - core)
+    own_rows = pl.multiple_of((x * 2 + core) * ROWS, ROWS)
+    own_cols = pl.multiple_of(core * 2 * UNITS_PAD, 2 * UNITS_PAD)
+    resid_copy = pltpu.make_async_copy(residual.at[pl.ds(own_rows, ROWS), :], resid, local_sem.at[0])
+    resid_copy.start()
+    weight_copy = pltpu.make_async_copy(
+        weights_hbm, weights.at[:, pl.ds(own_cols, 2 * UNITS_PAD)], local_sem.at[1]
+    )
+    weight_copy.start()
+    greet(x, y, z, core)
+
+    halves = []
+    for chip in range(4):
+        rows = pl.multiple_of((chip * 2 + 1 - core) * ROWS, ROWS)
+        copy = remote(
+            projected.at[pl.ds(rows, ROWS), :], half.at[chip], half_send.at[chip], half_recv.at[chip], sibling
+        )
+        copy.start()
+        halves.append(copy)
+    sums = []
+    for steps in (2, 1, 3):
+        chip = lax.rem(x + steps, 4)
+        rows = pl.multiple_of((chip * 2 + core) * ROWS, ROWS)
+        if steps == 2:
+            for copy in halves:
+                copy.wait_recv()
+        summed[steps] = (
+            projected[pl.ds(rows, ROWS), :].astype(jnp.float32) + half[chip].astype(jnp.float32)
+        ).astype(jnp.bfloat16)
+        copy = remote(
+            summed.at[steps],
+            arrived.at[steps],
+            sum_send.at[steps - 1],
+            sum_recv.at[steps - 1],
+            device(*ahead(here, 0, steps), core),
+        )
+        copy.start()
+        sums.append(copy)
+    swap = remote(
+        weights_hbm, weights.at[:, pl.ds(own_cols, 2 * UNITS_PAD)], weight_sem.at[0], weight_sem.at[1], sibling
+    )
+    swap.start()
+    total = projected[pl.ds(own_rows, ROWS), :].astype(jnp.float32) + half[x].astype(jnp.float32)
+    for copy in sums:
+        copy.wait_recv()
+    for steps in (1, 2, 3):
+        total = total + arrived[steps].astype(jnp.float32)
+    resid_copy.wait()
+    stream = (resid[...].astype(jnp.float32) + total).astype(jnp.bfloat16)
+    stream_out[...] = stream
+    tokens[x, y, z] = normed_rows(stream.astype(jnp.float32), gain[...])
+
+    def block(part, phase, coords, first, width):
+        order = PARTS[part][2]
+        index = list(coords)
+        for axis in order[:phase]:
+            index[axis] = slice(None)
+        return tokens.at[index[0], index[1], index[2], :, pl.ds(first, width)]
+
+    pending = []
+    for phase in range(3):
+        direct = []
+        for part, (first, width, order) in enumerate(PARTS):
+            axis = order[phase]
+            src = block(part, phase, here, first, width)
+            pair = []
+            for way, steps in enumerate((1, 3)):
+                copy = remote(
+                    src,
+                    src,
+                    part_send.at[part, phase, way],
+                    part_recv.at[part, phase, way],
+                    device(*ahead(here, axis, steps), core),
+                )
+                copy.start()
+                pair.append(copy)
+            direct.append(pair)
+        onward = []
+        for part, (first, width, order) in enumerate(PARTS):
+            axis = order[phase]
+            cut = 896
+            for way, (steps, start, size) in enumerate(((1, first, cut), (3, first + cut, width - cut))):
+                direct[part][way].wait_recv()
+                src = block(part, phase, ahead(here, axis, 4 - steps), start, size)
+                copy = remote(
+                    src,
+                    src,
+                    part_send.at[part, phase, 2 + way],
+                    part_recv.at[part, phase, 2 + way],
+                    device(*ahead(here, axis, steps), core),
+                )
+                copy.start()
+                onward.append(copy)
+        for copy in onward:
+            copy.wait_recv()
+        pending += [copy for pair in direct for copy in pair] + onward
+
+    weight_copy.wait()
+    swap.wait_recv()
+
+    @pl.loop(0, 4)
+    def _(step):
+        chip = lax.rem(x + 3 - step, 4)
+        for line in range(4):
+            rows = tokens[chip, line].reshape(4 * ROWS, MODEL)
+            both = jnp.dot(rows, weights[...], preferred_element_type=jnp.float32)
+            outs = []
+            for which in range(2):
+                gate = both[:, which * 2 * UNITS_PAD : which * 2 * UNITS_PAD + UNITS_PAD]
+                upper = both[:, which * 2 * UNITS_PAD + UNITS_PAD : (which + 1) * 2 * UNITS_PAD]
+                outs.append((gate / (1.0 + jnp.exp(-gate)) * upper).astype(jnp.bfloat16))
+            hidden[chip, pl.ds(line * 4 * ROWS, 4 * ROWS), :] = jnp.concatenate(outs, axis=1)
+
+    spot = hidden_out.at[:, pl.ds(pl.multiple_of(x * 2 * UNITS_PAD, 2 * UNITS_PAD), 2 * UNITS_PAD)]
+    for steps in (2, 1, 3):
+        target = ahead(here, 0, steps)
+        copy = remote(
+            hidden.at[target[0]], spot, hid_send.at[steps - 1], hid_recv.at[steps - 1], device(*target, core)
+        )
+        copy.start()
+        pending.append(copy)
+        copy_list = copy
+        sums.append(copy_list)
+    own_hidden = pltpu.make_async_copy(hidden.at[x], spot, local_sem.at[2])
+    own_hidden.start()
+    own_hidden.wait()
+    for copy in sums[3:]:
+        copy.wait_recv()
+    for copy in halves + sums[:3] + [swap] + pending:
+        copy.wait_send()
+
+
+def spread(projected, residual, gain, weights):
+    vmem = pl.BlockSpec(memory_space=pltpu.VMEM)
+    anywhere = pl.BlockSpec(memory_space=pl.ANY)
+    return pl.pallas_call(
+        spread_kernel,
+        out_shape=(
+            jax.ShapeDtypeStruct((ROWS, MODEL), jnp.bfloat16),
+            jax.ShapeDtypeStruct((256, 8 * UNITS_PAD), jnp.bfloat16),
+        ),
+        in_specs=[vmem, anywhere, vmem, anywhere],
+        out_specs=(vmem, anywhere),
+        scratch_shapes=[
+            pltpu.VMEM((ROWS, MODEL), jnp.bfloat16),
+            pltpu.VMEM((4, ROWS, MODEL), jnp.bfloat16),
+            pltpu.VMEM((4, ROWS, MODEL), jnp.bfloat16),
+            pltpu.VMEM((4, ROWS, MODEL), jnp.bfloat16),
+            pltpu.VMEM((4, 4, 4, ROWS, MODEL), jnp.bfloat16),
+            pltpu.VMEM((MODEL, 4 * UNITS_PAD), jnp.bfloat16),
+            pltpu.VMEM((4, 256, 2 * UNITS_PAD), jnp.bfloat16),
+            pltpu.SemaphoreType.DMA((3,)),
+            pltpu.SemaphoreType.DMA((4,)),
+            pltpu.SemaphoreType.DMA((4,)),
+            pltpu.SemaphoreType.DMA((3,)),
+            pltpu.SemaphoreType.DMA((3,)),
+            pltpu.SemaphoreType.DMA((2,)),
+            pltpu.SemaphoreType.DMA((3, 3, 4)),
+            pltpu.SemaphoreType.DMA((3, 3, 4)),
+            pltpu.SemaphoreType.DMA((3,)),
+            pltpu.SemaphoreType.DMA((3,)),
+        ],
+        compiler_params=pltpu.CompilerParams(
+            collective_id=0, has_side_effects=True, vmem_limit_bytes=48 << 20
+        ),
+        cost_estimate=pl.CostEstimate(flops=2 * 1024 * 5120 * 512, bytes_accessed=200 << 20, transcendentals=0),
+    )(projected, residual, gain, weights)
+
+
+CHUNKS = 4
+
+
+def gather_kernel(
+    hidden_hbm,
+    down_hbm,
+    stream,
+    gain,
+    qkv_hbm,
+    bias,
+    layer_out,
+    qkv_out,
+    hidden,
+    down,
+    qkv,
+    partial,
+    first_in,
+    second,
+    second_in,
+    rows,
+    local_sem,
+    down_sem,
+    first_send,
+    first_recv,
+    second_send,
+    second_recv,
+    row_send,
+    row_recv,
+):
+    x, y, z, core = place()
+    here = (x, y, z)
+    sibling = device(x, y, z, 1 - core)
+    hidden_copy = pltpu.make_async_copy(hidden_hbm, hidden, local_sem.at[0])
+    hidden_copy.start()
+    down_copies = []
+    for member in range(8):
+        copy = pltpu.make_async_copy(
+            down_hbm.at[member], down.at[member, pl.ds(0, DOWN_PAD), :], down_sem.at[member]
+        )
+        copy.start()
+        down_copies.append(copy)
+    qkv_copy = pltpu.make_async_copy(qkv_hbm, qkv, local_sem.at[1])
+    qkv_copy.start()
+    for member in range(8):
+        down[member, pl.ds(DOWN_PAD, UNITS_PAD - DOWN_PAD), :] = jnp.zeros(
+            (UNITS_PAD - DOWN_PAD, MODEL), jnp.bfloat16
+        )
+    greet(x, y, z, core)
+    hidden_copy.wait()
+    for copy in down_copies:
+        copy.wait()
+
+    size = MODEL // CHUNKS
+    sent = []
+    firsts = []
+    for chunk in range(CHUNKS):
+        cols = pl.ds(chunk * size, size)
+        total = jnp.dot(
+            hidden[...],
+            down[:, :, chunk * size : (chunk + 1) * size].reshape(8 * UNITS_PAD, size),
+            preferred_element_type=jnp.float32,
+        )
+        partial[:, :, :, cols] = total.astype(jnp.bfloat16).reshape(4, 4, ROWS, size)
+        axis = 1 + chunk % 2
+        copies = []
+        for steps in (2, 1, 3):
+            target = ahead(here, axis, steps)
+            src = partial.at[target[1], :, :, cols] if axis == 1 else partial.at[:, target[2], :, cols]
+            copy = remote(
+                src,
+                first_in.at[chunk, steps - 1],
+                first_send.at[chunk, steps - 1],
+                first_recv.at[chunk, steps - 1],
+                device(*target, core),
+            )
+            copy.start()
+            copies.append(copy)
+        firsts.append(copies)
+        sent += copies
+    seconds = []
+    for chunk in range(CHUNKS):
+        cols = pl.ds(chunk * size, size)
+        axis = 1 + chunk % 2
+        for copy in firsts[chunk]:
+            copy.wait_recv()
+        own = partial[y, :, :, cols] if axis == 1 else partial[:, z, :, cols]
+        total = own.astype(jnp.float32)
+        for steps in range(3):
+            total = total + first_in[chunk, steps].astype(jnp.float32)
+        second[chunk] = total.astype(jnp.bfloat16)
+        copies = []
+        for steps in (2, 1, 3):
+            target = ahead(here, 3 - axis, steps)
+            copy = remote(
+                second.at[chunk, target[3 - axis]],
+                second_in.at[chunk, steps - 1],
+                second_send.at[chunk, steps - 1],
+                second_recv.at[chunk, steps - 1],
+                device(*target, core),
+            )
+            copy.start()
+            copies.append(copy)
+        seconds.append(copies)
+        sent += copies
+    parts = []
+    for chunk in range(CHUNKS):
+        axis = 1 + chunk % 2
+        for copy in seconds[chunk]:
+            copy.wait_recv()
+        total = second[chunk, here[3 - axis]].astype(jnp.float32)
+        for steps in range(3):
+            total = total + second_in[chunk, steps].astype(jnp.float32)
+        parts.append(total)
+    mixed = jnp.concatenate(parts, axis=1)
+    out = (stream[...].astype(jnp.float32) + mixed).astype(jnp.bfloat16)
+    layer_out[...] = out
+    mine = x * 2 + core
+    rows[mine] = normed_rows(out.astype(jnp.float32), gain[...])
+    ring = []
+    for steps in (2, 1, 3):
+        copy = remote(
+            rows.at[mine],
+            rows.at[mine],
+            row_send.at[steps - 1],
+            row_recv.at[steps - 1],
+            device(*ahead(here, 0, steps), core),
+        )
+        copy.start()
+        ring.append((steps, copy))
+    twins = []
+    copy = remote(rows.at[mine], rows.at[mine], row_send.at[3], row_recv.at[3], sibling)
+    copy.start()
+    twins.append(copy)
+    for steps, arrival in reversed(ring):
+        arrival.wait_recv()
+        other = lax.rem(x + 4 - steps, 4) * 2 + core
+        copy = remote(rows.at[other], rows.at[other], row_send.at[3 + steps], row_recv.at[3 + steps], sibling)
+        copy.start()
+        twins.append(copy)
+    for copy in twins:
+        copy.wait_recv()
+    qkv_copy.wait()
+    result = jnp.dot(rows[...].reshape(8 * ROWS, MODEL), qkv[...], preferred_element_type=jnp.float32)
+    qkv_out[...] = (result + bias[...]).astype(jnp.bfloat16)
+    for copy in sent + [copy for _, copy in ring] + twins:
+        copy.wait_send()
+
+
+def gather(hidden, down, stream, gain, qkv, bias):
+    vmem = pl.BlockSpec(memory_space=pltpu.VMEM)
+    anywhere = pl.BlockSpec(memory_space=pl.ANY)
+    size = MODEL // CHUNKS
+    return pl.pallas_call(
+        gather_kernel,
+        out_shape=(
+            jax.ShapeDtypeStruct((ROWS, MODEL), jnp.bfloat16),
+            jax.ShapeDtypeStruct((8 * ROWS, QKV_COLS), jnp.bfloat16),
+        ),
+        in_specs=[anywhere, anywhere, vmem, vmem, anywhere, vmem],
+        out_specs=(vmem, vmem),
+        scratch_shapes=[
+            pltpu.VMEM((256, 8 * UNITS_PAD), jnp.bfloat16),
+            pltpu.VMEM((8, UNITS_PAD, MODEL), jnp.bfloat16),
+            pltpu.VMEM((MODEL, QKV_COLS), jnp.bfloat16),
+            pltpu.VMEM((4, 4, ROWS, MODEL), jnp.bfloat16),
+            pltpu.VMEM((CHUNKS, 3, 4, ROWS, size), jnp.bfloat16),
+            pltpu.VMEM((CHUNKS, 4, ROWS, size), jnp.bfloat16),
+            pltpu.VMEM((CHUNKS, 3, ROWS, size), jnp.bfloat16),
+            pltpu.VMEM((8, ROWS, MODEL), jnp.bfloat16),
+            pltpu.SemaphoreType.DMA((2,)),
+            pltpu.SemaphoreType.DMA((8,)),
+            pltpu.SemaphoreType.DMA((CHUNKS, 3)),
+            pltpu.SemaphoreType.DMA((CHUNKS, 3)),
+            pltpu.SemaphoreType.DMA((CHUNKS, 3)),
+            pltpu.SemaphoreType.DMA((CHUNKS, 3)),
+            pltpu.SemaphoreType.DMA((7,)),
+            pltpu.SemaphoreType.DMA((7,)),
+        ],
+        compiler_params=pltpu.CompilerParams(
+            collective_id=1, has_side_effects=True, vmem_limit_bytes=48 << 20
+        ),
+        cost_estimate=pl.CostEstimate(flops=2 * 256 * 5120 * 1024, bytes_accessed=100 << 20, transcendentals=0),
+    )(hidden, down, stream, gain, qkv, bias)
+
+
 def body(
     queries,
     leaf_keys,
@@ -119,6 +549,10 @@
     qkv_proj,
     qkv_bias,
 ):
+    down_padded = jnp.pad(down_proj, ((0, DOWN_PAD - UNITS), (0, 0)))
+    down_all = lax.all_gather(down_padded, "mlp", axis=0, tiled=False)
+    lanes = ((0, 0), (0, UNITS_PAD - UNITS))
+    weights = jnp.concatenate([jnp.pad(gate_proj, lanes), jnp.pad(up_proj, lanes)], axis=1)
     prefix = fetch_prefix(key_value_pages, page_holder, page_slot)
     attention = attend(
         queries,
@@ -131,40 +565,9 @@
         mid_parent[0],
         node_len[0],
     )
-    projected = jnp.dot(attention, out_proj, preferred_element_type=jnp.float32)
-    group_tokens = queries.shape[0]
-    groups = lax.axis_size("req")
-    members = lax.axis_size("mlp")
-    rows_mlp = group_tokens // members
-    first_row = lax.axis_index("mlp") * rows_mlp
-    head_part = lax.psum_scatter(
-        projected.astype(jnp.bfloat16), "mlp", scatter_dimension=0, tiled=True
-    ).astype(jnp.float32)
-    own_resid = lax.dynamic_slice_in_dim(residual, first_row, rows_mlp, 0)
-    stream = (own_resid.astype(jnp.float32) + head_part).astype(jnp.bfloat16)
-    normed = rms_norm(stream, norm_gain)
-    piece = lax.all_gather(normed, ("req", "mlp"), axis=0, tiled=True)
-    gate = jnp.dot(piece, gate_proj, preferred_element_type=jnp.float32)
-    upper = jnp.dot(piece, up_proj, preferred_element_type=jnp.float32)
-    hidden_all = (jax.nn.silu(gate) * upper).astype(jnp.bfloat16)
-    blocks = hidden_all.reshape(groups, members, rows_mlp, -1)
-    regrouped = lax.all_to_all(blocks, "mlp", split_axis=1, concat_axis=3, tiled=True)
-    hidden = regrouped.reshape(groups * rows_mlp, -1)
-    mixed_all = jnp.dot(
-        hidden,
-        lax.all_gather(down_proj, "mlp", axis=0, tiled=True),
-        preferred_element_type=jnp.float32,
-    )
-    mixed = lax.psum_scatter(
-        mixed_all.astype(jnp.bfloat16), "req", scatter_dimension=0, tiled=True
-    ).astype(jnp.float32)
-    layer_out = (stream.astype(jnp.float32) + mixed).astype(jnp.bfloat16)
-    next_rows = rms_norm(layer_out, next_gain)
-    next_normed = lax.all_gather(next_rows, "mlp", axis=0, tiled=True)
-    qkv_out = (
-        jnp.dot(next_normed, qkv_proj, preferred_element_type=jnp.float32) + qkv_bias
-    ).astype(jnp.bfloat16)
-    return (layer_out, qkv_out)
+    projected = jnp.dot(attention, out_proj, preferred_element_type=jnp.float32).astype(jnp.bfloat16)
+    stream, hidden = spread(projected, residual, norm_gain.reshape(1, -1), weights)
+    return gather(hidden, down_all, stream, next_gain.reshape(1, -1), qkv_proj, qkv_bias.reshape(1, -1))
 
 
 def solution(mesh):

time: 357 us -> 186 us (0.52)
  waiting for transfers between devices: 254 us -> 0.04 us
  Pallas kernels: 0 us -> 132 us
  matrix products: 39 us -> 3.29 us
  local copies, waits for them, and re-layouts: 24.3 us -> 19.3 us
  starting transfers between devices: 13.2 us -> 8.64 us
    all_gather x3 -> x1, waiting for transfers between devices: 149 us -> 0.02 us  [body(): down_all = lax.all_gather(down_padded, 'mlp', axis=0, tiled=False)]
    pallas_call x0 -> x2, Pallas kernels: none -> 132 us  [the longest x1 92.5 us: spread(): pl.pallas_call(spread_kernel, out_shape=(jax.ShapeDtypeStruct((ROWS, MODE...]
    reduce_scatter x2 -> x0, waiting for transfers between devices: 105 us -> none  [the longest x1 73.7 us: body(): lax.psum_scatter(mixed_all.astype(jnp.bfloat16), 'req', scatter_dimension...]
    dot_general x5 -> x1, matrix products: 36.9 us -> 1.24 us  [body(): jnp.dot(attention, out_proj, preferred_element_type=jnp.float32)]
    all_to_all x1 -> x0, starting transfers between devices: 4.27 us -> none  [body(): lax.all_to_all(blocks, 'mlp', split_axis=1, concat_axis=3, tiled=True)]
    unnamed x33 -> x38, local copies, waits for them, and re-layouts: 10.9 us -> 7.83 us
  transfers between devices with their start and end apart: 7 -> 2, of which waited for: 5 -> 0; matrix products, arithmetic and copies ran while one was open for 11% -> 14% of each run, Pallas kernels for 0% -> 50%
where the time goes in v1:
time: 186 us
  Pallas kernels  132 us (71%)
  local copies, waits for them, and re-layouts  19.3 us (10%)
  between operations  14.4 us (8%)
  starting transfers between devices  8.64 us (5%)
  other arithmetic  8.51 us (5%)
  matrix products  3.29 us (2%)
    pallas_call x1, Pallas kernels, spread(): pl.pallas_call(spread_kernel, out_shape=(jax.ShapeDtypeStruct((ROWS, MODE...  92.5 us
    pallas_call x1, Pallas kernels, gather(): pl.pallas_call(gather_kernel, out_shape=(jax.ShapeDtypeStruct((ROWS, MODE...  39.2 us
    all_to_all x1, starting transfers between devices, fetch_prefix(): lax.all_to_all(outgoing, 'req', split_axis=0, concat_axis=0, tiled=True)  8.6 us
    unnamed x38, local copies, waits for them, and re-layouts  7.83 us
  transfers between devices with their start and end apart: 2, of which 0 were waited for; matrix products, arithmetic and copies ran while one was open for 14% of the time, Pallas kernels for 50%

profile of v1, /device:TPU:1, one launch (start us, length us, event | category | flops | bytes accessed | tf_op | source)
XLA Modules:
  0.0 185.9 jit_solution(7523125694192327342)
XLA Ops:
  7.2 0.0 copy-start
  7.2 0.0 copy-start.6
  7.2 0.0 copy-start.9
  7.2 0.0 copy-start.5
  7.2 0.0 all-gather.3.cloned.1.call-start
  7.3 2.4 %pad.13 = bf16[112,5120]{1,0:T(8,128)(2,1)} pad(bf16[108,5120]{1,0:T(8,128)(2,1)} %param.34, bf16[]{:T(256)} %constant.55.clone.1), padding=0_4x0_0 | pad | bytes 2252802 | tf_op jit(solution)/shard_map/jit(_pad)/pad | solution.py:552
  9.7 0.0 all-gather.3.cloned.1.call-update
  9.7 0.8 copy.70
  10.5 0.4 convert_reduce_fusion
  11.0 0.1 copy.75
  11.1 0.8 select_reduce_fusion
  11.8 0.0 copy-done
  11.9 2.4 %gather_fusion.1 = bf16[16,64,2,128]{3,2,1,0:T(2,128)(2,1)} fusion(bf16[32,64,2,128]{3,2,1,0:T(2,128)(2,1)S(1)} %copy-done, s32[1024]{0:T(1024)S(1)} %pad_clamp_fusion.1), kind=kCustom, calls=%fused_computation.1 | custom fusion | bytes 1048640 | tf_op jit(solution)/shard_map/gather | solution.py:93
  14.2 8.6 %all-to-all-start = ((bf16[16,1,64,2,128]{4,3,2,1,0:T(2,128)(2,1)}), bf16[16,1,64,2,128]{4,3,2,1,0:T(2,128)(2,1)S(1)}, u32[]{:S(2)}, u32[]{:S(2)}) async-start(bf16[16,1,64,2,128]{4,3,2,1,0:T(2,128)(2,1)} %bitcast.9), calls=%async_computation | async-start | bytes 1048576 | tf_op jit(solution)/shard_map/all_to_all | solution.py:94
  22.8 0.0 copy-start.7
  22.9 0.0 copy-start.8
  22.9 0.0 copy-start.12
  22.9 0.0 copy-start.13
  22.9 0.1 broadcast_in_dim.28
  23.0 0.1 broadcast_in_dim.29
  23.1 0.0 copy-done.6
  23.1 0.1 constant_dynamic-slice_fusion.1
  23.1 0.1 copy.87
  23.2 2.1 %gather_fusion = bf16[24,64,2,128]{3,2,1,0:T(2,128)(2,1)S(1)} fusion(bf16[32,64,2,128]{3,2,1,0:T(2,128)(2,1)S(1)} %copy-done, s32[1024]{0:T(1024)S(1)} %pad_clamp_fusion.2), kind=kCustom, calls=%fused_computation | custom fusion | bytes 1572960 | tf_op jit(solution)/shard_map/gather | solution.py:100
  25.4 1.1 copy.72
  26.5 0.0 copy-done.9
  26.5 0.1 iota_compare_fusion.4
  26.6 0.0 copy-done.5
  26.6 0.2 copy.77
  26.8 1.8 copy.81
  28.6 2.5 %copy.82 = bf16[5120,108]{1,0:T(8,128)(2,1)} copy(bf16[5120,108]{0,1:T(8,128)(2,1)} %param.33) | data formatting | bytes 2211840 | tf_op args[14]
  31.1 0.0 copy-done.7
  31.1 0.0 copy-done.8
  31.2 0.0 copy-done.12
  31.2 0.1 select_reduce_fusion.1
  31.3 0.0 copy-done.13
  31.3 0.1 select_reduce_fusion.2
  31.3 0.1 fusion.24
  31.4 1.1 or_and_fusion
  32.5 3.3 %fusion.5.weights_hbm = bf16[5120,256]{1,0:T(8,128)(2,1)} fusion(bf16[5120,108]{1,0:T(8,128)(2,1)} %copy.82, bf16[5120,108]{1,0:T(8,128)(2,1)S(1)} %copy.81), kind=kLoop, calls=%fused_computation.13 | loop fusion | flops 10485760 | bytes 4833280 | tf_op jit(solution)/shard_map/concatenate | solution.py:555
  35.8 0.0 all-to-all-done
  35.9 2.1 %gather_fusion.2 = bf16[24,64,2,128]{3,2,1,0:T(2,128)(2,1)S(1)} fusion(bf16[16,64,2,128]{3,2,1,0:T(2,128)(2,1)S(1)} %bitcast.90, s32[1024]{0:T(1024)S(1)} %pad_clamp_fusion), kind=kCustom, calls=%fused_computation.2 | custom fusion | bytes 1572960 | tf_op jit(solution)/shard_map/gather | solution.py:99
  38.0 0.2 copy.76
  38.2 1.5 bitcast_select_fusion.1
  39.7 0.1 fusion.38
  39.7 0.0 copy-done.10
  39.7 0.0 copy-start.11
  39.7 0.8 fusion.2
  40.5 0.0 slice-start
  40.5 1.0 fusion.3
  41.6 0.0 copy-done.11
  41.6 0.0 slice-start.1
  41.6 1.3 fusion.16
  42.9 0.0 slice-done
  42.9 0.9 slice-done.1
  43.8 1.2 convolution_convert_fusion.projected
  45.0 0.5 copy-done.1
  45.6 0.4 copy-done.3
  45.9 0.0 copy-done.4
  45.9 92.5 %shard_map.194 = (bf16[16,5120]{1,0:T(8,128)(2,1)S(1)}, bf16[256,1024]{1,0:T(8,128)(2,1)S(1)}) custom-call(bf16[128,5120]{1,0:T(8,128)(2,1)S(1)} %convolution_convert_fusion.projected, bf16[128,5120]{1,0:T(8,128)(2,1)S(1)} %copy-done.3, f32[1,5120]{1,0:T(1,128)S(1)} %bitcast.86, bf16[5120,256]{1,0:T(8,128)(2,1)S(1)} %copy-done.1), custom_call_target="tpu_custom_call" | custom-call | flops 5368709120 | bytes 209715200 | tf_op jit(solution)/shard_map/pallas_call | solution.py:312
  138.4 0.0 all-gather.3.cloned.1.call-done
  138.4 39.2 %shard_map.195 = (bf16[16,5120]{1,0:T(8,128)(2,1)S(1)}, bf16[128,896]{1,0:T(8,128)(2,1)S(1)}) custom-call(bf16[256,1024]{1,0:T(8,128)(2,1)S(1)} %get-tuple-element.4.hidden_hbm, bf16[8,112,5120]{2,1,0:T(8,128)(2,1)} %bitcast.89, bf16[16,5120]{1,0:T(8,128)(2,1)S(1)} %get-tuple-element.5.stream, f32[1,5120]{1,0:T(1,128)S(1)} %bitcast.85, ...), custom_call_target="tpu_custom_call" | custom-call | flops 2684354560 | bytes 104857600 | tf_op jit(solution)/shard_map/pallas_call | solution.py:498
  177.7 0.7 copy.90
  178.3 0.7 copy.91
  (22 shorter events, 0.1 us)
Async XLA Ops:
  7.2 4.7 %copy-start = (bf16[32,64,2,128]{3,2,1,0:T(2,128)(2,1)S(1)}, bf16[32,64,2,128]{3,2,1,0:T(2,128)(2,1)}, u32[]{:S(2)}) copy-start(bf16[32,64,2,128]{3,2,1,0:T(2,128)(2,1)} %param.22) | copy-start | bytes 3145732
  7.2 15.9 %copy-start.6 = (s32[16,6,4]{0,2,1:T(4,128)S(1)}, s32[16,6,4]{0,2,1:T(4,128)}, u32[]{:S(2)}) copy-start(s32[16,6,4]{0,2,1:T(4,128)} %param.24) | copy-start | bytes 4612
  7.2 19.3 %copy-start.9 = (s32[1,6]{1,0:T(1,128)S(1)}, s32[1,6]{1,0:T(1,128)}, u32[]{:S(2)}) copy-start(s32[1,6]{1,0:T(1,128)} %param.28) | copy-start | bytes 76
  7.2 19.4 %copy-start.5 = (bf16[128,640]{1,0:T(8,128)(2,1)S(1)}, bf16[128,640]{1,0:T(8,128)(2,1)}, u32[]{:S(2)}) copy-start(bf16[128,640]{1,0:T(8,128)(2,1)} %param.19) | copy-start | bytes 491524
  7.2 131.2 %all-gather.3.cloned.1.call-start = ((), (), s32[]{:S(2)}) async-start(), calls=%async_computation.1 | async-start | bytes 10321920 | tf_op jit(solution)/shard_map/all_gather | solution.py:553
  14.2 21.6 %all-to-all-start = ((bf16[16,1,64,2,128]{4,3,2,1,0:T(2,128)(2,1)}), bf16[16,1,64,2,128]{4,3,2,1,0:T(2,128)(2,1)S(1)}, u32[]{:S(2)}, u32[]{:S(2)}) async-start(bf16[16,1,64,2,128]{4,3,2,1,0:T(2,128)(2,1)} %bitcast.9), calls=%async_computation | async-start | bytes 1048576 | tf_op jit(solution)/shard_map/all_to_all | solution.py:94
  22.8 8.3 %copy-start.7 = (f32[896]{0:T(1024)S(1)}, f32[896]{0:T(1024)}, u32[]{:S(2)}) copy-start(f32[896]{0:T(1024)} %param.37) | copy-start | bytes 10756
  22.9 8.3 %copy-start.8 = (s32[128]{0:T(128)S(1)}, s32[128]{0:T(128)}, u32[]{:S(2)}) copy-start(s32[128]{0:T(128)} %param.25) | copy-start | bytes 1540
  22.9 8.3 %copy-start.12 = (s32[1,8]{1,0:T(1,128)S(1)}, s32[1,8]{1,0:T(1,128)}, u32[]{:S(2)}) copy-start(s32[1,8]{1,0:T(1,128)} %param.26) | copy-start | bytes 100
  22.9 8.4 %copy-start.13 = (s32[1,4]{1,0:T(1,128)S(1)}, s32[1,4]{1,0:T(1,128)}, u32[]{:S(2)}) copy-start(s32[1,4]{1,0:T(1,128)} %param.27) | copy-start | bytes 52
  35.8 3.9 %copy-start.10 = (bf16[128,128]{1,0:T(8,128)(2,1)S(1)}, bf16[128,128]{1,0:T(8,128)(2,1)}, u32[]{:S(2)}) copy-start(bf16[128,128]{1,0:T(8,128)(2,1)} %param.20) | copy-start | bytes 98308
  39.7 1.9 %copy-start.11 = (bf16[128,128]{1,0:T(8,128)(2,1)S(1)}, bf16[128,128]{1,0:T(8,128)(2,1)}, u32[]{:S(2)}) copy-start(bf16[128,128]{1,0:T(8,128)(2,1)} %param.21) | copy-start | bytes 98308
  40.5 2.3 %slice-start = ((s8[6553600]{0:T(1024)(128)(4,1)}), s8[4194304]{0:T(1024)(128)(4,1)S(1)}, s32[]{:S(2)}) async-start(s8[6553600]{0:T(1024)(128)(4,1)} %bitcast.87), calls=%async_computation.2 | async-start | bytes 8388608
  41.6 2.2 %slice-start.1 = ((s8[6553600]{0:T(1024)(128)(4,1)}), s8[2359296]{0:T(1024)(128)(4,1)S(1)}, s32[]{:S(2)}) async-start(s8[6553600]{0:T(1024)(128)(4,1)} %bitcast.87), calls=%async_computation.3 | async-start | bytes 4718592
  43.8 1.8 copy-start.1
  43.8 2.2 %copy-start.3 = (bf16[128,5120]{1,0:T(8,128)(2,1)S(1)}, bf16[128,5120]{1,0:T(8,128)(2,1)}, u32[]{:S(2)}) copy-start(bf16[128,5120]{1,0:T(8,128)(2,1)} %residual.1) | copy-start | bytes 3932164
  43.8 2.2 %copy-start.4 = (f32[5120]{0:T(1024)S(1)}, f32[5120]{0:T(1024)}, u32[]{:S(2)}) copy-start(f32[5120]{0:T(1024)} %param.31) | copy-start | bytes 61444
  45.9 92.5 %copy-start.2 = (f32[5120]{0:T(1024)S(1)}, f32[5120]{0:T(1024)}, u32[]{:S(2)}) copy-start(f32[5120]{0:T(1024)} %param.35) | copy-start | bytes 61444
Sparse Core Ops, SparseCore 0:
  9.8 63.6 all-gather.2

commit v2 on v0

v2 whole, which is shorter than its diff:
```python
import functools
import math

import jax
import jax.numpy as jnp
from jax import lax
from jax.experimental import pallas as pl
from jax.experimental.pallas import tpu as pltpu
from jax.sharding import PartitionSpec as P

HEAD_SIZE = 128
QUERY_PER_KV = 5
REQ_DEV = 8
ROOT_DEV = 2
MID_DEV = 4
NODES_DEV = 6
NODE_MAX = 256
MODEL = 5120
ROWS = 16
UNITS = 108
UNITS_PAD = 128
DOWN_PAD = 112
QKV_COLS = 896
TOKENS = 128
PAGES = 32
PAGE = 64
ENTRIES = 24
PREFIX = NODES_DEV * NODE_MAX
SLICES = 4
CHUNKS = 4
HIDDEN = -1e30

EPS = 1e-06

MESH = pl.DeviceIdType.MESH


def place():
    req = lax.axis_index("req")
    mlp = lax.axis_index("mlp")
    return lax.div(mlp, 2), lax.div(req, 4), lax.rem(req, 4), lax.rem(mlp, 2)


def device(x, y, z, core):
    return (y * 4 + z, x * 2 + core)


def ahead(coords, axis, steps):
    moved = list(coords)
    moved[axis] = lax.rem(moved[axis] + steps, 4)
    return moved


def greet(others):
    barrier = pltpu.get_barrier_semaphore()
    for other in others:
        pl.semaphore_signal(barrier, inc=1, device_id=other, device_id_type=MESH)


def greeted(others):
    pl.semaphore_wait(pltpu.get_barrier_semaphore(), len(others))


def lines_through(x, y, z, core):
    others = [device(x, y, z, 1 - core)]
    for axis in range(3):
        for steps in (1, 2, 3):
            others.append(device(*ahead((x, y, z), axis, steps), core))
    return others


def remote(src, dst, send, recv, target):
    return pltpu.make_async_remote_copy(
        src_ref=src, dst_ref=dst, send_sem=send, recv_sem=recv, device_id=target, device_id_type=MESH
    )


def normed_rows(rows, gain):
    mean_sq = jnp.mean(rows * rows, axis=-1, keepdims=True)
    return (rows * lax.rsqrt(mean_sq + EPS) * gain).astype(jnp.bfloat16)


PARTS = (
    (0, 640, 256, (1, 2, 0)),
    (640, 2048, 1024, (2, 0, 1)),
    (2688, 2432, 1280, (0, 1, 2)),
)


def layer_kernel(
    queries,
    leaf_keys,
    leaf_values,
    pages_hbm,
    holder,
    slot,
    segment_row,
    req_parent,
    mid_parent,
    node_len,
    residual,
    out_hbm,
    gain,
    gate_hbm,
    up_hbm,
    down_hbm,
    next_gain,
    qkv_hbm,
    bias,
    layer_out,
    qkv_out,
    pages,
    outgoing,
    incoming,
    keys,
    values,
    hide,
    attention,
    out_proj,
    gate_up,
    own_down,
    projected,
    resid,
    half,
    summed,
    arrived,
    tokens,
    weights,
    hidden,
    hidden_in,
    sums_f32,
    down,
    qkv,
    first_in,
    second,
    second_in,
    rows,
    local_sem,
    page_send,
    page_recv,
    half_send,
    half_recv,
    sum_send,
    sum_recv,
    weight_sem,
    part_send,
    part_recv,
    hid_send,
    hid_recv,
    down_send,
    down_recv,
    twin_send,
    twin_recv,
    first_send,
    first_recv,
    second_send,
    second_recv,
    row_send,
    row_recv,
):
    x, y, z, core = place()
    here = (x, y, z)
    group = lax.axis_index("req")
    sibling = device(x, y, z, 1 - core)
    own_rows = pl.multiple_of((x * 2 + core) * ROWS, ROWS)
    own_cols = pl.multiple_of(core * 2 * UNITS_PAD, 2 * UNITS_PAD)
    mine = x * 2 + core
    others = lines_through(x, y, z, core)
    plane = []
    for offset in range(1, 16):
        spot = (x, lax.rem(y + offset // 4, 4), lax.rem(z + offset % 4, 4))
        plane.append(spot)
        if offset // 4 and offset % 4:
            others.append(device(*spot, core))
    greet(others)

    def local(src, dst, index):
        copy = pltpu.make_async_copy(src, dst, local_sem.at[index])
        copy.start()
        return copy

    pages_copy = local(pages_hbm, pages, 0)
    gate_copy = local(gate_hbm, gate_up.at[0], 1)
    up_copy = local(up_hbm, gate_up.at[1], 2)
    down_copy = local(down_hbm, own_down, 5)
    out_copy = local(out_hbm, out_proj, 3)
    resid_copy = local(residual.at[pl.ds(own_rows, ROWS), :], resid, 4)
    qkv_copy = local(qkv_hbm, qkv, 6)

    pages_copy.wait()
    for number, spot in enumerate(plane):
        asker = spot[1] * 4 + spot[2]
        picked = jnp.int32(0)
        for entry in range(ENTRIES):
            picked = jnp.where(holder[entry // 4, entry % 4, asker] == group, slot[entry // 4, entry % 4, asker], picked)
        outgoing[number] = pages[picked]
    greeted(others)
    fetched = []
    for number in range(14, -1, -1):
        copy = remote(
            outgoing.at[number],
            incoming.at[group],
            page_send.at[number],
            page_recv.at[number],
            device(*plane[number], core),
        )
        copy.start()
        fetched.append(copy)

    gate_copy.wait()
    up_copy.wait()
    for which in range(2):
        cols = pl.ds(pl.multiple_of(own_cols + which * UNITS_PAD, UNITS_PAD), UNITS_PAD)
        weights[:, cols] = jnp.concatenate(
            [gate_up[which], jnp.zeros((UNITS_PAD - UNITS, MODEL), jnp.bfloat16)], axis=0
        ).T
    spot = weights.at[:, pl.ds(own_cols, 2 * UNITS_PAD)]
    swap = remote(spot, spot, weight_sem.at[0], weight_sem.at[1], sibling)
    swap.start()

    twins = []
    downs = []

    def down_block(offset, first, width):
        member = lax.rem(x + offset, 4) * 2 + core
        return down.at[member, pl.ds(0, DOWN_PAD), pl.ds(first, width)]

    def down_push(kind, part, way, offset, first, width):
        view = down_block(offset, first, width)
        copy = remote(
            view,
            view,
            down_send.at[kind, part, way],
            down_recv.at[kind, part, way],
            device(*ahead(here, 0, (1, 3)[way]), core),
        )
        copy.start()
        downs.append(copy)
        return copy

    def twin(offset):
        view = down_block(offset, 0, MODEL)
        copy = remote(view, view, twin_send.at[offset], twin_recv.at[offset], sibling)
        copy.start()
        twins.append(copy)

    wide = MODEL // 2

    def down_direct(part):
        return [down_push(0, part, way, 0, part * wide, wide) for way in range(2)]

    def down_onward(part):
        return [
            down_push(1, part, way, behind, part * wide + way * (wide // 2), wide // 2)
            for way, behind in enumerate((3, 1))
        ]

    down_copy.wait()
    down[mine, pl.ds(0, DOWN_PAD), :] = jnp.concatenate(
        [own_down[...], jnp.zeros((DOWN_PAD - UNITS, MODEL), jnp.bfloat16)], axis=0
    )
    for member in range(8):
        down[member, pl.ds(DOWN_PAD, UNITS_PAD - DOWN_PAD), :] = jnp.zeros(
            (UNITS_PAD - DOWN_PAD, MODEL), jnp.bfloat16
        )
    down_near = [down_direct(0)]
    twin(0)

    line = segment_row[...]
    across = lax.broadcasted_iota(jnp.int32, (TOKENS, TOKENS), 1)
    along = lax.broadcasted_iota(jnp.int32, (TOKENS, TOKENS), 0)
    segments = jnp.sum(jnp.where(across == along, line, 0), axis=1, keepdims=True)
    middle = jnp.zeros_like(segments)
    for request in range(REQ_DEV):
        middle = jnp.where(segments == request, req_parent[0, request], middle)
    root = jnp.zeros_like(segments)
    for node in range(MID_DEV):
        root = jnp.where(middle == node, mid_parent[0, node], root)
    position = lax.broadcasted_iota(jnp.int32, (TOKENS, NODE_MAX), 1)
    for node in range(NODES_DEV):
        chosen = root == node if node < ROOT_DEV else middle == node - ROOT_DEV
        length = jnp.where(chosen, node_len[0, node], 0)
        hide[:, node * NODE_MAX : (node + 1) * NODE_MAX] = jnp.where(position < length, 0.0, HIDDEN)
    hide[:, PREFIX:] = jnp.where((segments == line) & (across <= along), 0.0, HIDDEN)

    for copy in fetched:
        copy.wait_recv()
    for entry in range(ENTRIES):
        kept = holder[entry // 4, entry % 4, group]
        page = jnp.where(kept == group, pages[slot[entry // 4, entry % 4, group]], incoming[kept])
        keys[entry * PAGE : (entry + 1) * PAGE, :] = page[:, :HEAD_SIZE]
        values[entry * PAGE : (entry + 1) * PAGE, :] = page[:, HEAD_SIZE:]
    keys[PREFIX:, :] = leaf_keys[...]
    values[PREFIX:, :] = leaf_values[...]
    for head in range(QUERY_PER_KV):
        cols = slice(head * HEAD_SIZE, (head + 1) * HEAD_SIZE)
        score = lax.dot_general(
            queries[:, cols], keys[...], (((1,), (1,)), ((), ())), preferred_element_type=jnp.float32
        )
        score = score * (1.0 / math.sqrt(HEAD_SIZE)) + hide[...]
        expo = jnp.exp(score - jnp.max(score, axis=1, keepdims=True))
        total = jnp.sum(expo, axis=1, keepdims=True)
        seen = jnp.dot(expo.astype(jnp.bfloat16), values[...], preferred_element_type=jnp.float32)
        attention[:, cols] = (seen / total).astype(jnp.bfloat16)

    out_copy.wait()
    size = MODEL // SLICES
    halves = []
    for piece in range(SLICES):
        cols = slice(piece * size, (piece + 1) * size)
        term = jnp.dot(attention[...], out_proj[:, cols], preferred_element_type=jnp.float32)
        term = term.astype(jnp.bfloat16).reshape(4, 2, ROWS, size)
        projected[0, :, :, cols] = term[:, 0]
        projected[1, :, :, cols] = term[:, 1]
        copy = remote(
            projected.at[1 - core, :, :, cols],
            half.at[:, :, cols],
            half_send.at[piece],
            half_recv.at[piece],
            sibling,
        )
        copy.start()
        halves.append(copy)
    sums = []
    for piece in range(SLICES):
        cols = slice(piece * size, (piece + 1) * size)
        halves[piece].wait_recv()
        for steps in (2, 1, 3):
            chip = lax.rem(x + steps, 4)
            summed[steps, :, cols] = (
                projected[core, chip, :, cols].astype(jnp.float32) + half[chip, :, cols].astype(jnp.float32)
            ).astype(jnp.bfloat16)
            copy = remote(
                summed.at[steps, :, cols],
                arrived.at[steps, :, cols],
                sum_send.at[piece, steps - 1],
                sum_recv.at[piece, steps - 1],
                device(*ahead(here, 0, steps), core),
            )
            copy.start()
            sums.append(copy)
    total = projected[core, x].astype(jnp.float32) + half[x].astype(jnp.float32)
    down_far = []
    for copy in down_near[0]:
        copy.wait_recv()
    down_far += down_onward(0)
    for copy in sums:
        copy.wait_recv()
    for steps in (1, 2, 3):
        total = total + arrived[steps].astype(jnp.float32)
    resid_copy.wait()
    stream = (resid[...].astype(jnp.float32) + total).astype(jnp.bfloat16)
    tokens[x, y, z] = normed_rows(stream.astype(jnp.float32), gain[...])

    def block(part, offsets, half=None):
        first, width, cut, order = PARTS[part]
        if half is not None:
            first, width = ((first, cut), (first + cut, width - cut))[half]
        index = [slice(None)] * 3
        for axis, offset in zip(order, offsets):
            if offset is not None:
                index[axis] = lax.rem(here[axis] + offset, 4)
        return (index[0], index[1], index[2], slice(None), pl.ds(first, width))

    pending = []

    def push(part, phase, slot, way, spot):
        view = tokens.at[spot]
        copy = remote(
            view,
            view,
            part_send.at[part, phase, slot, way],
            part_recv.at[part, phase, slot, way],
            device(*ahead(here, PARTS[part][3][phase], (1, 3)[way]), core),
        )
        copy.start()
        pending.append(copy)
        return copy

    def both_ways(part, phase, slot, offsets):
        spot = block(part, offsets)
        return [push(part, phase, slot, way, spot) for way in range(2)]

    def onward(part, phase, slot, offsets):
        return [
            push(part, phase, slot, way, block(part, offsets[:phase] + (behind,) + offsets[phase + 1 :], way))
            for way, behind in enumerate((3, 1))
        ]

    def arrive(copies):
        for copy in copies:
            copy.wait_recv()

    def product(part, offset):
        first, width, _, order = PARTS[part]
        index = [slice(None)] * 3
        index[order[2]] = lax.rem(here[order[2]] + offset, 4)
        rows = tokens[index[0], index[1], index[2], :, pl.ds(first, width)].reshape(256, width)
        term = jnp.dot(rows, weights[pl.ds(first, width), :], preferred_element_type=jnp.float32)
        spot = (index[0], index[1], index[2])
        shape = [4, 4, 4]
        del shape[order[2]]
        sums_f32[spot] += term.reshape(*shape, ROWS, 4 * UNITS_PAD)

    every = range(3)
    near = [both_ways(part, 0, 0, (0, 0, 0)) for part in every]
    lines = [both_ways(part, 1, 0, (0, 0, 0)) for part in every]
    down_near.append(down_direct(1))
    sums_f32[...] = jnp.zeros_like(sums_f32)
    far = []
    for part in every:
        arrive(near[part])
        far.append(onward(part, 0, 1, (0, 0, 0)))
        for slot, offset in ((1, 1), (2, 3)):
            lines[part] += both_ways(part, 1, slot, (offset, 0, 0))
    planes = [[None] * 4 for _ in every]
    for part in every:
        arrive(far[part])
        lines[part] += both_ways(part, 1, 3, (2, 0, 0))
        planes[part][0] = both_ways(part, 2, 0, (None, 0, 0))
    far = []
    for part in every:
        arrive(lines[part])
        far.append(onward(part, 1, 4, (None, 0, 0)))
        for offset in (1, 3):
            planes[part][offset] = both_ways(part, 2, offset, (None, offset, 0))
    for part in every:
        arrive(far[part])
        planes[part][2] = both_ways(part, 2, 2, (None, 2, 0))
    swap.wait_recv()
    arrive(down_near[1])
    down_far += down_onward(1)
    twin(1)
    twin(3)
    last = []
    for offset in (0, 1, 3, 2):
        for part in every:
            arrive(planes[part][offset])
            last += onward(part, 2, 4 + offset, (None, offset, 0))
        if offset in (0, 1, 3):
            product((0, 1, None, 2)[offset], 0)
    for part in every:
        product(part, 1)
        product(part, 3)
    arrive(down_far)
    twin(2)
    arrive(last)
    for part in every:
        product(part, 2)

    given = []
    spot = hidden_in.at[:, pl.ds(pl.multiple_of(x * 2 * UNITS_PAD, 2 * UNITS_PAD), 2 * UNITS_PAD)]
    for steps in (2, 1, 3, 0):
        target = ahead(here, 0, steps)
        chip = target[0]
        both = sums_f32[chip].reshape(256, 4 * UNITS_PAD)
        outs = []
        for which in range(2):
            gate = both[:, which * 2 * UNITS_PAD : which * 2 * UNITS_PAD + UNITS_PAD]
            upper = both[:, which * 2 * UNITS_PAD + UNITS_PAD : (which + 1) * 2 * UNITS_PAD]
            outs.append((gate / (1.0 + jnp.exp(-gate)) * upper).astype(jnp.bfloat16))
        if steps:
            hidden[steps - 1] = jnp.concatenate(outs, axis=1)
            copy = remote(
                hidden.at[steps - 1], spot, hid_send.at[steps - 1], hid_recv.at[steps - 1], device(*target, core)
            )
            copy.start()
            given.append(copy)
        else:
            spot[...] = jnp.concatenate(outs, axis=1)
    for copy in pending:
        copy.wait_send()
    partial = tokens.at[0]
    arrive(given)
    arrive(twins)

    size = MODEL // CHUNKS
    sent = []
    firsts = []
    for chunk in range(CHUNKS):
        cols = pl.ds(chunk * size, size)
        total = jnp.dot(
            hidden_in[...],
            down[:, :, chunk * size : (chunk + 1) * size].reshape(8 * UNITS_PAD, size),
            preferred_element_type=jnp.float32,
        )
        partial[:, :, :, cols] = total.astype(jnp.bfloat16).reshape(4, 4, ROWS, size)
        axis = 1 + chunk % 2
        copies = []
        for steps in (2, 1, 3):
            target = ahead(here, axis, steps)
            src = partial.at[target[1], :, :, cols] if axis == 1 else partial.at[:, target[2], :, cols]
            copy = remote(
                src,
                first_in.at[chunk, steps - 1],
                first_send.at[chunk, steps - 1],
                first_recv.at[chunk, steps - 1],
                device(*target, core),
            )
            copy.start()
            copies.append(copy)
        firsts.append(copies)
        sent += copies
    seconds = []
    for chunk in range(CHUNKS):
        cols = pl.ds(chunk * size, size)
        axis = 1 + chunk % 2
        for copy in firsts[chunk]:
            copy.wait_recv()
        own = partial[y, :, :, cols] if axis == 1 else partial[:, z, :, cols]
        total = own.astype(jnp.float32)
        for steps in range(3):
            total = total + first_in[chunk, steps].astype(jnp.float32)
        second[chunk] = total.astype(jnp.bfloat16)
        copies = []
        for steps in (2, 1, 3):
            target = ahead(here, 3 - axis, steps)
            copy = remote(
                second.at[chunk, target[3 - axis]],
                second_in.at[chunk, steps - 1],
                second_send.at[chunk, steps - 1],
                second_recv.at[chunk, steps - 1],
                device(*target, core),
            )
            copy.start()
            copies.append(copy)
        seconds.append(copies)
        sent += copies
    parts = []
    for chunk in range(CHUNKS):
        axis = 1 + chunk % 2
        for copy in seconds[chunk]:
            copy.wait_recv()
        total = second[chunk, here[3 - axis]].astype(jnp.float32)
        for steps in range(3):
            total = total + second_in[chunk, steps].astype(jnp.float32)
        parts.append(total)
    mixed = jnp.concatenate(parts, axis=1)
    out = (stream.astype(jnp.float32) + mixed).astype(jnp.bfloat16)
    layer_out[...] = out
    rows[mine] = normed_rows(out.astype(jnp.float32), next_gain[...])
    ring = []
    for steps in (2, 1, 3):
        copy = remote(
            rows.at[mine],
            rows.at[mine],
            row_send.at[steps - 1],
            row_recv.at[steps - 1],
            device(*ahead(here, 0, steps), core),
        )
        copy.start()
        ring.append((steps, copy))
    passed = []
    copy = remote(rows.at[mine], rows.at[mine], row_send.at[3], row_recv.at[3], sibling)
    copy.start()
    passed.append(copy)
    for steps, arrival in reversed(ring):
        arrival.wait_recv()
        other = lax.rem(x + 4 - steps, 4) * 2 + core
        copy = remote(rows.at[other], rows.at[other], row_send.at[3 + steps], row_recv.at[3 + steps], sibling)
        copy.start()
        passed.append(copy)
    for copy in passed:
        copy.wait_recv()
    qkv_copy.wait()
    result = jnp.dot(rows[...].reshape(8 * ROWS, MODEL), qkv[...], preferred_element_type=jnp.float32)
    qkv_out[...] = (result + bias[...]).astype(jnp.bfloat16)
    for copy in fetched + halves + sums + [swap] + downs + twins + given + sent + [copy for _, copy in ring] + passed:
        copy.wait_send()


def layer(*operands):
    vmem = pl.BlockSpec(memory_space=pltpu.VMEM)
    smem = pl.BlockSpec(memory_space=pltpu.SMEM)
    anywhere = pl.BlockSpec(memory_space=pl.ANY)
    dma = pltpu.SemaphoreType.DMA

    def held(*shape):
        return pltpu.VMEM(shape, jnp.bfloat16)

    size = MODEL // CHUNKS
    return pl.pallas_call(
        layer_kernel,
        out_shape=(
            jax.ShapeDtypeStruct((ROWS, MODEL), jnp.bfloat16),
            jax.ShapeDtypeStruct((TOKENS, QKV_COLS), jnp.bfloat16),
        ),
        in_specs=[vmem] * 3
        + [anywhere, smem, smem, vmem, smem, smem, smem, anywhere, anywhere, vmem]
        + [anywhere, anywhere, anywhere, vmem, anywhere, vmem],
        out_specs=(vmem, vmem),
        scratch_shapes=[
            held(PAGES, PAGE, 2 * HEAD_SIZE),
            held(15, PAGE, 2 * HEAD_SIZE),
            held(16, PAGE, 2 * HEAD_SIZE),
            held(PREFIX + TOKENS, HEAD_SIZE),
            held(PREFIX + TOKENS, HEAD_SIZE),
            pltpu.VMEM((TOKENS, PREFIX + TOKENS), jnp.float32),
            held(TOKENS, QUERY_PER_KV * HEAD_SIZE),
            held(QUERY_PER_KV * HEAD_SIZE, MODEL),
            held(2, UNITS, MODEL),
            held(UNITS, MODEL),
            held(2, 4, ROWS, MODEL),
            held(ROWS, MODEL),
            held(4, ROWS, MODEL),
            held(4, ROWS, MODEL),
            held(4, ROWS, MODEL),
            held(4, 4, 4, ROWS, MODEL),
            held(MODEL, 4 * UNITS_PAD),
            held(3, 256, 2 * UNITS_PAD),
            held(256, 8 * UNITS_PAD),
            pltpu.VMEM((4, 4, 4, ROWS, 4 * UNITS_PAD), jnp.float32),
            held(8, UNITS_PAD, MODEL),
            held(MODEL, QKV_COLS),
            held(CHUNKS, 3, 4, ROWS, size),
            held(CHUNKS, 4, ROWS, size),
            held(CHUNKS, 3, ROWS, size),
            held(8, ROWS, MODEL),
            dma((7,)),
            dma((15,)),
            dma((15,)),
            dma((SLICES,)),
            dma((SLICES,)),
            dma((SLICES, 3)),
            dma((SLICES, 3)),
            dma((2,)),
            dma((3, 3, 8, 2)),
            dma((3, 3, 8, 2)),
            dma((3,)),
            dma((3,)),
            dma((2, 2, 2)),
            dma((2, 2, 2)),
            dma((4,)),
            dma((4,)),
            dma((CHUNKS, 3)),
            dma((CHUNKS, 3)),
            dma((CHUNKS, 3)),
            dma((CHUNKS, 3)),
            dma((7,)),
            dma((7,)),
        ],
        compiler_params=pltpu.CompilerParams(
            collective_id=0, has_side_effects=True, vmem_limit_bytes=63 << 20
        ),
        cost_estimate=pl.CostEstimate(flops=2 * 1024 * 5120 * 512, bytes_accessed=200 << 20, transcendentals=0),
    )(*operands)


def body(
    queries,
    leaf_keys,
    leaf_token_values,
    key_value_pages,
    page_holder,
    page_slot,
    segment_ids,
    req_parent,
    mid_parent,
    node_len,
    residual,
    out_proj,
    norm_gain,
    gate_proj,
    up_proj,
    down_proj,
    next_gain,
    qkv_proj,
    qkv_bias,
):
    return layer(
        queries,
        leaf_keys,
        leaf_token_values,
        key_value_pages.reshape(PAGES, PAGE, 2 * HEAD_SIZE),
        page_holder.transpose(1, 2, 0),
        page_slot.transpose(1, 2, 0),
        segment_ids.reshape(1, TOKENS),
        req_parent,
        mid_parent,
        node_len,
        residual,
        out_proj,
        norm_gain.reshape(1, -1),
        gate_proj.T,
        up_proj.T,
        down_proj,
        next_gain.reshape(1, -1),
        qkv_proj,
        qkv_bias.reshape(1, -1),
    )


def solution(mesh):
    placed = (
        P("req", "mlp"),
        P("req", "mlp"),
        P("req", "mlp"),
        P("req", None, None, "mlp"),
        P(),
        P(),
        P("req"),
        P("req", None),
        P("req", None),
        P("req", None),
        P("req", None),
        P("mlp", None),
        P(),
        P(None, ("req", "mlp")),
        P(None, ("req", "mlp")),
        P(("req", "mlp"), None),
        P(),
        P(None, "mlp"),
        P("mlp"),
    )
    return jax.shard_map(
        body,
        mesh=mesh,
        in_specs=placed,
        out_specs=(P(("req", "mlp"), None), P("req", "mlp")),
        check_vma=False,
    )
```

time: 357 us -> 154 us (0.43)
  waiting for transfers between devices: 254 us -> 0 us
  Pallas kernels: 0 us -> 146 us
  matrix products: 39 us -> 0 us
  local copies, waits for them, and re-layouts: 24.3 us -> 7.03 us
  between operations: 14.1 us -> 0.64 us
  starting transfers between devices: 13.2 us -> 0 us
  other arithmetic: 11.4 us -> 0 us
    all_gather x3 -> x0, waiting for transfers between devices: 149 us -> none  [the longest x1 90.1 us: body(): piece = lax.all_gather(normed, ('req', 'mlp'), axis=0, tiled=True)]
    pallas_call x0 -> x1, Pallas kernels: none -> 146 us  [layer(): pl.pallas_call(layer_kernel, out_shape=(jax.ShapeDtypeStruct((ROWS, MODEL...]
    reduce_scatter x2 -> x0, waiting for transfers between devices: 105 us -> none  [the longest x1 73.7 us: body(): lax.psum_scatter(mixed_all.astype(jnp.bfloat16), 'req', scatter_dimension...]
    dot_general x7 -> x0, matrix products: 39 us -> none  [the longest x1 13.8 us: body(): gate = jnp.dot(piece, gate_proj, preferred_element_type=jnp.float32)]
    all_to_all x2 -> x0, starting transfers between devices: 12.9 us -> none  [the longest x1 8.6 us: fetch_prefix(): lax.all_to_all(outgoing, 'req', split_axis=0, concat_axis=0, tiled=True)]
    gather x5 -> x0, local copies, waits for them, and re-layouts: 9.44 us -> none  [the longest x1 3.59 us: fetch_prefix(): outgoing = key_value_pages[send_slot]]
    unnamed x33 -> x2, local copies, waits for them, and re-layouts: 10.9 us -> 3.24 us
    reduce_sum x7 -> x0, other arithmetic: 5.98 us -> none  [the longest x2 2.25 us: rms_norm(): mean_sq = jnp.mean(values * values, axis=-1, keepdims=True)]
  transfers between devices with their start and end apart: 7 -> 0, of which waited for: 5 -> 0; matrix products, arithmetic and copies ran while one was open for 11% -> 0% of each run, Pallas kernels for 0% -> 0%
where the time goes in v2:
time: 154 us
  Pallas kernels  146 us (95%)
  local copies, waits for them, and re-layouts  7.03 us (5%)
    pallas_call x1, Pallas kernels, layer(): pl.pallas_call(layer_kernel, out_shape=(jax.ShapeDtypeStruct((ROWS, MODEL...  146 us
    unnamed x2, local copies, waits for them, and re-layouts  3.24 us

profile of v2, /device:TPU:1, one launch (start us, length us, event | category | flops | bytes accessed | tf_op | source)
XLA Modules:
  0.0 153.6 jit_solution(3274302997626130533)
XLA Ops:
  0.6 1.3 reshape.23.bias
  1.9 2.5 %reshape.19.pages_hbm = bf16[32,64,256]{2,1,0:T(8,128)(2,1)} reshape(bf16[32,64,2,128]{3,2,1,0:T(2,128)(2,1)} %param.22) | data formatting | bytes 2097152 | tf_op jit(solution)/shard_map/reshape | solution.py:674
  4.4 145.9 %shard_map.194 = (bf16[16,5120]{1,0:T(8,128)(2,1)}, bf16[128,896]{1,0:T(8,128)(2,1)}) custom-call(bf16[128,640]{1,0:T(8,128)(2,1)} %queries.1, bf16[128,128]{1,0:T(8,128)(2,1)} %leaf_keys.1, bf16[128,128]{1,0:T(8,128)(2,1)} %leaf_values.1, bf16[32,64,256]{2,1,0:T(8,128)(2,1)} %reshape.19.pages_hbm, s32[6,4,16]{2,1,0:T(4,128)} %bitcast.11, ...), custom_call_target="tpu_custom_call" | custom-call | flops 5368709120 | bytes 209715200 | tf_op jit(solution)/shard_map/pallas_call | solution.py:582
  150.4 1.6 %copy.23 = bf16[16,5120]{1,0:T(8,128)(2,1)} copy(bf16[16,5120]{1,0:T(8,128)(2,1)} %get-tuple-element.4) | data formatting | bytes 327680
  152.0 1.6 %copy.24 = bf16[128,896]{1,0:T(8,128)(2,1)} copy(bf16[128,896]{1,0:T(8,128)(2,1)} %get-tuple-element.5) | data formatting | bytes 458752

commit v3 on v2

--- a/solution.py
+++ b/solution.py
@@ -81,9 +81,9 @@
 
 
 PARTS = (
-    (0, 640, 256, (1, 2, 0)),
-    (640, 2048, 1024, (2, 0, 1)),
-    (2688, 2432, 1280, (0, 1, 2)),
+    (0, 1024, 512, (1, 2, 0)),
+    (1024, 2048, 1024, (0, 1, 2)),
+    (3072, 2048, 1024, (0, 2, 1)),
 )
 
 
@@ -264,7 +264,6 @@
             (UNITS_PAD - DOWN_PAD, MODEL), jnp.bfloat16
         )
     down_near = [down_direct(0)]
-    twin(0)
 
     line = segment_row[...]
     across = lax.broadcasted_iota(jnp.int32, (TOKENS, TOKENS), 1)
@@ -340,10 +339,6 @@
             copy.start()
             sums.append(copy)
     total = projected[core, x].astype(jnp.float32) + half[x].astype(jnp.float32)
-    down_far = []
-    for copy in down_near[0]:
-        copy.wait_recv()
-    down_far += down_onward(0)
     for copy in sums:
         copy.wait_recv()
     for steps in (1, 2, 3):
@@ -405,7 +400,7 @@
     every = range(3)
     near = [both_ways(part, 0, 0, (0, 0, 0)) for part in every]
     lines = [both_ways(part, 1, 0, (0, 0, 0)) for part in every]
-    down_near.append(down_direct(1))
+    twin(0)
     sums_f32[...] = jnp.zeros_like(sums_f32)
     far = []
     for part in every:
@@ -418,6 +413,9 @@
         arrive(far[part])
         lines[part] += both_ways(part, 1, 3, (2, 0, 0))
         planes[part][0] = both_ways(part, 2, 0, (None, 0, 0))
+    arrive(down_near[0])
+    down_far = down_onward(0)
+    down_near.append(down_direct(1))
     far = []
     for part in every:
         arrive(lines[part])
@@ -428,10 +426,6 @@
         arrive(far[part])
         planes[part][2] = both_ways(part, 2, 2, (None, 2, 0))
     swap.wait_recv()
-    arrive(down_near[1])
-    down_far += down_onward(1)
-    twin(1)
-    twin(3)
     last = []
     for offset in (0, 1, 3, 2):
         for part in every:
@@ -439,6 +433,11 @@
             last += onward(part, 2, 4 + offset, (None, offset, 0))
         if offset in (0, 1, 3):
             product((0, 1, None, 2)[offset], 0)
+        if offset == 1:
+            arrive(down_near[1])
+            down_far += down_onward(1)
+            twin(1)
+            twin(3)
     for part in every:
         product(part, 1)
         product(part, 3)

time: 154 us -> 134 us (0.87)
  Pallas kernels: 146 us -> 126 us
    pallas_call x1, Pallas kernels: 146 us -> 126 us  [layer(): pl.pallas_call(layer_kernel, out_shape=(jax.ShapeDtypeStruct((ROWS, MODEL...]
where the time goes in v3:
time: 134 us
  Pallas kernels  126 us (94%)
  local copies, waits for them, and re-layouts  7.03 us (5%)
    pallas_call x1, Pallas kernels, layer(): pl.pallas_call(layer_kernel, out_shape=(jax.ShapeDtypeStruct((ROWS, MODEL...  126 us
    unnamed x2, local copies, waits for them, and re-layouts  3.24 us

profile of v3, /device:TPU:1, one launch (start us, length us, event | category | flops | bytes accessed | tf_op | source)
XLA Modules:
  0.0 133.7 jit_solution(13078476716532309522)
XLA Ops:
  0.6 1.3 reshape.23.bias
  1.9 2.5 %reshape.19.pages_hbm = bf16[32,64,256]{2,1,0:T(8,128)(2,1)} reshape(bf16[32,64,2,128]{3,2,1,0:T(2,128)(2,1)} %param.22) | data formatting | bytes 2097152 | tf_op jit(solution)/shard_map/reshape | solution.py:673
  4.4 126.0 %shard_map.194 = (bf16[16,5120]{1,0:T(8,128)(2,1)}, bf16[128,896]{1,0:T(8,128)(2,1)}) custom-call(bf16[128,640]{1,0:T(8,128)(2,1)} %queries.1, bf16[128,128]{1,0:T(8,128)(2,1)} %leaf_keys.1, bf16[128,128]{1,0:T(8,128)(2,1)} %leaf_values.1, bf16[32,64,256]{2,1,0:T(8,128)(2,1)} %reshape.19.pages_hbm, s32[6,4,16]{2,1,0:T(4,128)} %bitcast.11, ...), custom_call_target="tpu_custom_call" | custom-call | flops 5368709120 | bytes 209715200 | tf_op jit(solution)/shard_map/pallas_call | solution.py:581
  130.4 1.6 %copy.23 = bf16[16,5120]{1,0:T(8,128)(2,1)} copy(bf16[16,5120]{1,0:T(8,128)(2,1)} %get-tuple-element.4) | data formatting | bytes 327680
  132.0 1.6 %copy.24 = bf16[128,896]{1,0:T(8,128)(2,1)} copy(bf16[128,896]{1,0:T(8,128)(2,1)} %get-tuple-element.5) | data formatting | bytes 458752

commit v4 on v3

--- a/solution.py
+++ b/solution.py
@@ -26,7 +26,7 @@
 PAGE = 64
 ENTRIES = 24
 PREFIX = NODES_DEV * NODE_MAX
-SLICES = 4
+SLICES = 5
 CHUNKS = 4
 HIDDEN = -1e30
 
@@ -125,12 +125,12 @@
     summed,
     arrived,
     tokens,
-    weights,
+    wide_weights,
     hidden,
     hidden_in,
     sums_f32,
+    squares,
     down,
-    qkv,
     first_in,
     second,
     second_in,
@@ -165,6 +165,7 @@
     own_rows = pl.multiple_of((x * 2 + core) * ROWS, ROWS)
     own_cols = pl.multiple_of(core * 2 * UNITS_PAD, 2 * UNITS_PAD)
     mine = x * 2 + core
+    weights = wide_weights.at[:, 0 : 4 * UNITS_PAD]
     others = lines_through(x, y, z, core)
     plane = []
     for offset in range(1, 16):
@@ -180,12 +181,11 @@
         return copy
 
     pages_copy = local(pages_hbm, pages, 0)
+    down_copy = local(down_hbm, own_down, 5)
     gate_copy = local(gate_hbm, gate_up.at[0], 1)
     up_copy = local(up_hbm, gate_up.at[1], 2)
-    down_copy = local(down_hbm, own_down, 5)
     out_copy = local(out_hbm, out_proj, 3)
     resid_copy = local(residual.at[pl.ds(own_rows, ROWS), :], resid, 4)
-    qkv_copy = local(qkv_hbm, qkv, 6)
 
     pages_copy.wait()
     for number, spot in enumerate(plane):
@@ -206,17 +206,6 @@
         )
         copy.start()
         fetched.append(copy)
-
-    gate_copy.wait()
-    up_copy.wait()
-    for which in range(2):
-        cols = pl.ds(pl.multiple_of(own_cols + which * UNITS_PAD, UNITS_PAD), UNITS_PAD)
-        weights[:, cols] = jnp.concatenate(
-            [gate_up[which], jnp.zeros((UNITS_PAD - UNITS, MODEL), jnp.bfloat16)], axis=0
-        ).T
-    spot = weights.at[:, pl.ds(own_cols, 2 * UNITS_PAD)]
-    swap = remote(spot, spot, weight_sem.at[0], weight_sem.at[1], sibling)
-    swap.start()
 
     twins = []
     downs = []
@@ -324,6 +313,7 @@
     for piece in range(SLICES):
         cols = slice(piece * size, (piece + 1) * size)
         halves[piece].wait_recv()
+        passing = []
         for steps in (2, 1, 3):
             chip = lax.rem(x + steps, 4)
             summed[steps, :, cols] = (
@@ -337,15 +327,22 @@
                 device(*ahead(here, 0, steps), core),
             )
             copy.start()
-            sums.append(copy)
-    total = projected[core, x].astype(jnp.float32) + half[x].astype(jnp.float32)
-    for copy in sums:
-        copy.wait_recv()
-    for steps in (1, 2, 3):
-        total = total + arrived[steps].astype(jnp.float32)
-    resid_copy.wait()
-    stream = (resid[...].astype(jnp.float32) + total).astype(jnp.bfloat16)
-    tokens[x, y, z] = normed_rows(stream.astype(jnp.float32), gain[...])
+            passing.append(copy)
+        sums.append(passing)
+    gate_copy.wait()
+    up_copy.wait()
+    for which in range(2):
+        cols = pl.ds(pl.multiple_of(own_cols + which * UNITS_PAD, UNITS_PAD), UNITS_PAD)
+        weights[:, cols] = jnp.concatenate(
+            [
+                (gate_up[which].astype(jnp.float32) * gain[...]).astype(jnp.bfloat16),
+                jnp.zeros((UNITS_PAD - UNITS, MODEL), jnp.bfloat16),
+            ],
+            axis=0,
+        ).T
+    spot = weights.at[:, pl.ds(own_cols, 2 * UNITS_PAD)]
+    swap = remote(spot, spot, weight_sem.at[0], weight_sem.at[1], sibling)
+    swap.start()
 
     def block(part, offsets, half=None):
         first, width, cut, order = PARTS[part]
@@ -391,17 +388,32 @@
         index = [slice(None)] * 3
         index[order[2]] = lax.rem(here[order[2]] + offset, 4)
         rows = tokens[index[0], index[1], index[2], :, pl.ds(first, width)].reshape(256, width)
-        term = jnp.dot(rows, weights[pl.ds(first, width), :], preferred_element_type=jnp.float32)
+        exact = rows.astype(jnp.float32)
+        square = jnp.broadcast_to(jnp.sum(exact * exact, axis=1, keepdims=True), (256, HEAD_SIZE))
+        term = jnp.dot(rows, wide_weights[pl.ds(first, width), 0 : 4 * UNITS_PAD], preferred_element_type=jnp.float32)
         spot = (index[0], index[1], index[2])
         shape = [4, 4, 4]
         del shape[order[2]]
         sums_f32[spot] += term.reshape(*shape, ROWS, 4 * UNITS_PAD)
+        squares[spot] += square.reshape(*shape, ROWS, HEAD_SIZE)
 
     every = range(3)
-    near = [both_ways(part, 0, 0, (0, 0, 0)) for part in every]
-    lines = [both_ways(part, 1, 0, (0, 0, 0)) for part in every]
-    twin(0)
+    near, lines = [], []
+    resid_copy.wait()
+    for piece in range(SLICES):
+        cols = slice(piece * size, (piece + 1) * size)
+        arrive(sums[piece])
+        total = projected[core, x, :, cols].astype(jnp.float32) + half[x, :, cols].astype(jnp.float32)
+        for steps in (1, 2, 3):
+            total = total + arrived[steps, :, cols].astype(jnp.float32)
+        stream = (resid[:, cols].astype(jnp.float32) + total).astype(jnp.bfloat16)
+        resid[:, cols] = stream
+        tokens[x, y, z, :, cols] = stream
+        if piece % 2 == 0:
+            near.append(both_ways(piece // 2, 0, 0, (0, 0, 0)))
+            lines.append(both_ways(piece // 2, 1, 0, (0, 0, 0)))
     sums_f32[...] = jnp.zeros_like(sums_f32)
+    squares[...] = jnp.zeros_like(squares)
     far = []
     for part in every:
         arrive(near[part])
@@ -416,6 +428,7 @@
     arrive(down_near[0])
     down_far = down_onward(0)
     down_near.append(down_direct(1))
+    twin(0)
     far = []
     for part in every:
         arrive(lines[part])
@@ -447,12 +460,15 @@
     for part in every:
         product(part, 2)
 
+    swap.wait_send()
+    qkv_copy = local(qkv_hbm, wide_weights, 6)
     given = []
     spot = hidden_in.at[:, pl.ds(pl.multiple_of(x * 2 * UNITS_PAD, 2 * UNITS_PAD), 2 * UNITS_PAD)]
     for steps in (2, 1, 3, 0):
         target = ahead(here, 0, steps)
         chip = target[0]
-        both = sums_f32[chip].reshape(256, 4 * UNITS_PAD)
+        factor = lax.rsqrt(squares[chip].reshape(256, HEAD_SIZE)[:, :1] * (1.0 / MODEL) + EPS)
+        both = sums_f32[chip].reshape(256, 4 * UNITS_PAD) * factor
         outs = []
         for which in range(2):
             gate = both[:, which * 2 * UNITS_PAD : which * 2 * UNITS_PAD + UNITS_PAD]
@@ -535,36 +551,37 @@
             total = total + second_in[chunk, steps].astype(jnp.float32)
         parts.append(total)
     mixed = jnp.concatenate(parts, axis=1)
-    out = (stream.astype(jnp.float32) + mixed).astype(jnp.bfloat16)
+    out = (resid[...].astype(jnp.float32) + mixed).astype(jnp.bfloat16)
     layer_out[...] = out
     rows[mine] = normed_rows(out.astype(jnp.float32), next_gain[...])
     ring = []
-    for steps in (2, 1, 3):
-        copy = remote(
-            rows.at[mine],
-            rows.at[mine],
-            row_send.at[steps - 1],
-            row_recv.at[steps - 1],
-            device(*ahead(here, 0, steps), core),
+    passed = []
+
+    def hand(slot, member, part, target):
+        view = rows.at[member, :, pl.ds(part * wide, wide)]
+        copy = remote(view, view, row_send.at[part, slot], row_recv.at[part, slot], target)
+        copy.start()
+        return copy
+
+    for part in range(2):
+        ring.append([(steps, hand(steps - 1, mine, part, device(*ahead(here, 0, steps), core))) for steps in (2, 1, 3)])
+        passed.append([hand(3, mine, part, sibling)])
+    for part in range(2):
+        for steps, arrival in reversed(ring[part]):
+            arrival.wait_recv()
+            other = lax.rem(x + 4 - steps, 4) * 2 + core
+            passed[part].append(hand(3 + steps, other, part, sibling))
+    qkv_copy.wait()
+    result = bias[...].reshape(1, QKV_COLS)
+    for part in range(2):
+        arrive(passed[part])
+        result = result + jnp.dot(
+            rows[:, :, part * wide : (part + 1) * wide].reshape(TOKENS, wide),
+            wide_weights[part * wide : (part + 1) * wide, :],
+            preferred_element_type=jnp.float32,
         )
-        copy.start()
-        ring.append((steps, copy))
-    passed = []
-    copy = remote(rows.at[mine], rows.at[mine], row_send.at[3], row_recv.at[3], sibling)
-    copy.start()
-    passed.append(copy)
-    for steps, arrival in reversed(ring):
-        arrival.wait_recv()
-        other = lax.rem(x + 4 - steps, 4) * 2 + core
-        copy = remote(rows.at[other], rows.at[other], row_send.at[3 + steps], row_recv.at[3 + steps], sibling)
-        copy.start()
-        passed.append(copy)
-    for copy in passed:
-        copy.wait_recv()
-    qkv_copy.wait()
-    result = jnp.dot(rows[...].reshape(8 * ROWS, MODEL), qkv[...], preferred_element_type=jnp.float32)
-    qkv_out[...] = (result + bias[...]).astype(jnp.bfloat16)
-    for copy in fetched + halves + sums + [swap] + downs + twins + given + sent + [copy for _, copy in ring] + passed:
+    qkv_out[...] = result.astype(jnp.bfloat16)
+    for copy in fetched + halves + sum(sums, []) + downs + twins + given + sent + [copy for pair in ring for _, copy in pair] + sum(passed, []):
         copy.wait_send()
 
 
@@ -605,12 +622,12 @@
             held(4, ROWS, MODEL),
             held(4, ROWS, MODEL),
             held(4, 4, 4, ROWS, MODEL),
-            held(MODEL, 4 * UNITS_PAD),
+            held(MODEL, QKV_COLS),
             held(3, 256, 2 * UNITS_PAD),
             held(256, 8 * UNITS_PAD),
             pltpu.VMEM((4, 4, 4, ROWS, 4 * UNITS_PAD), jnp.float32),
+            pltpu.VMEM((4, 4, 4, ROWS, HEAD_SIZE), jnp.float32),
             held(8, UNITS_PAD, MODEL),
-            held(MODEL, QKV_COLS),
             held(CHUNKS, 3, 4, ROWS, size),
             held(CHUNKS, 4, ROWS, size),
             held(CHUNKS, 3, ROWS, size),
@@ -635,11 +652,11 @@
             dma((CHUNKS, 3)),
             dma((CHUNKS, 3)),
             dma((CHUNKS, 3)),
-            dma((7,)),
-            dma((7,)),
+            dma((2, 7)),
+            dma((2, 7)),
         ],
         compiler_params=pltpu.CompilerParams(
-            collective_id=0, has_side_effects=True, vmem_limit_bytes=63 << 20
+            collective_id=0, has_side_effects=True, vmem_limit_bytes=57 << 20
         ),
         cost_estimate=pl.CostEstimate(flops=2 * 1024 * 5120 * 512, bytes_accessed=200 << 20, transcendentals=0),
     )(*operands)
@@ -685,7 +702,7 @@
         down_proj,
         next_gain.reshape(1, -1),
         qkv_proj,
-        qkv_bias.reshape(1, -1),
+        qkv_bias,
     )
 
 

time: 134 us -> 130 us (0.970)
  Pallas kernels: 126 us -> 123 us
    pallas_call x1, Pallas kernels: 126 us -> 123 us  [layer(): pl.pallas_call(layer_kernel, out_shape=(jax.ShapeDtypeStruct((ROWS, MODEL...]
where the time goes in v4:
time: 130 us; the launch traced here: 129 us
  Pallas kernels  123 us (95%)
  local copies, waits for them, and re-layouts  5.77 us (4%)
    pallas_call x1, Pallas kernels, layer(): pl.pallas_call(layer_kernel, out_shape=(jax.ShapeDtypeStruct((ROWS, MODEL...  123 us
    unnamed x2, local copies, waits for them, and re-layouts  3.24 us

profile of v4, /device:TPU:1, one launch (start us, length us, event | category | flops | bytes accessed | tf_op | source)
XLA Modules:
  0.0 129.4 jit_solution(3174586234687770851)
XLA Ops:
  0.6 2.5 %reshape.16.pages_hbm = bf16[32,64,256]{2,1,0:T(8,128)(2,1)} reshape(bf16[32,64,2,128]{3,2,1,0:T(2,128)(2,1)} %param.22) | data formatting | bytes 2097152 | tf_op jit(solution)/shard_map/reshape | solution.py:690
  3.2 123.0 %shard_map.194 = (bf16[16,5120]{1,0:T(8,128)(2,1)}, bf16[128,896]{1,0:T(8,128)(2,1)}) custom-call(bf16[128,640]{1,0:T(8,128)(2,1)} %queries.1, bf16[128,128]{1,0:T(8,128)(2,1)} %leaf_keys.1, bf16[128,128]{1,0:T(8,128)(2,1)} %leaf_values.1, bf16[32,64,256]{2,1,0:T(8,128)(2,1)} %reshape.16.pages_hbm, s32[6,4,16]{2,1,0:T(4,128)} %bitcast.11, ...), custom_call_target="tpu_custom_call" | custom-call | flops 5368709120 | bytes 209715200 | tf_op jit(solution)/shard_map/pallas_call | solution.py:598
  126.1 1.6 %copy.23 = bf16[16,5120]{1,0:T(8,128)(2,1)} copy(bf16[16,5120]{1,0:T(8,128)(2,1)} %get-tuple-element.4) | data formatting | bytes 327680
  127.7 1.6 %copy.24 = bf16[128,896]{1,0:T(8,128)(2,1)} copy(bf16[128,896]{1,0:T(8,128)(2,1)} %get-tuple-element.5) | data formatting | bytes 458752

commit v5 on v4

--- a/solution.py
+++ b/solution.py
@@ -131,10 +131,6 @@
     sums_f32,
     squares,
     down,
-    first_in,
-    second,
-    second_in,
-    rows,
     local_sem,
     page_send,
     page_recv,
@@ -296,7 +292,10 @@
     halves = []
     for piece in range(SLICES):
         cols = slice(piece * size, (piece + 1) * size)
-        term = jnp.dot(attention[...], out_proj[:, cols], preferred_element_type=jnp.float32)
+        term = jnp.dot(
+            attention[...],
+            out_proj[:, :, cols].reshape(QUERY_PER_KV * HEAD_SIZE, size),
+            preferred_element_type=jnp.float32)
         term = term.astype(jnp.bfloat16).reshape(4, 2, ROWS, size)
         projected[0, :, :, cols] = term[:, 0]
         projected[1, :, :, cols] = term[:, 1]
@@ -486,6 +485,8 @@
     for copy in pending:
         copy.wait_send()
     partial = tokens.at[0]
+    rows = out_proj.at[0:8]
+    second = out_proj.at[8:12]
     arrive(given)
     arrive(twins)
 
@@ -507,7 +508,7 @@
             src = partial.at[target[1], :, :, cols] if axis == 1 else partial.at[:, target[2], :, cols]
             copy = remote(
                 src,
-                first_in.at[chunk, steps - 1],
+                out_proj.at[4 * steps + 8 : 4 * steps + 12, :, cols],
                 first_send.at[chunk, steps - 1],
                 first_recv.at[chunk, steps - 1],
                 device(*target, core),
@@ -525,14 +526,14 @@
         own = partial[y, :, :, cols] if axis == 1 else partial[:, z, :, cols]
         total = own.astype(jnp.float32)
         for steps in range(3):
-            total = total + first_in[chunk, steps].astype(jnp.float32)
-        second[chunk] = total.astype(jnp.bfloat16)
+            total = total + out_proj[4 * steps + 12 : 4 * steps + 16, :, cols].astype(jnp.float32)
+        second[:, :, cols] = total.astype(jnp.bfloat16)
         copies = []
         for steps in (2, 1, 3):
             target = ahead(here, 3 - axis, steps)
             copy = remote(
-                second.at[chunk, target[3 - axis]],
-                second_in.at[chunk, steps - 1],
+                second.at[target[3 - axis], :, cols],
+                out_proj.at[23 + steps, :, cols],
                 second_send.at[chunk, steps - 1],
                 second_recv.at[chunk, steps - 1],
                 device(*target, core),
@@ -546,9 +547,10 @@
         axis = 1 + chunk % 2
         for copy in seconds[chunk]:
             copy.wait_recv()
-        total = second[chunk, here[3 - axis]].astype(jnp.float32)
+        cols = pl.ds(chunk * size, size)
+        total = second[here[3 - axis], :, cols].astype(jnp.float32)
         for steps in range(3):
-            total = total + second_in[chunk, steps].astype(jnp.float32)
+            total = total + out_proj[24 + steps, :, cols].astype(jnp.float32)
         parts.append(total)
     mixed = jnp.concatenate(parts, axis=1)
     out = (resid[...].astype(jnp.float32) + mixed).astype(jnp.bfloat16)
@@ -613,7 +615,7 @@
             held(PREFIX + TOKENS, HEAD_SIZE),
             pltpu.VMEM((TOKENS, PREFIX + TOKENS), jnp.float32),
             held(TOKENS, QUERY_PER_KV * HEAD_SIZE),
-            held(QUERY_PER_KV * HEAD_SIZE, MODEL),
+            held(QUERY_PER_KV * HEAD_SIZE // ROWS, ROWS, MODEL),
             held(2, UNITS, MODEL),
             held(UNITS, MODEL),
             held(2, 4, ROWS, MODEL),
@@ -628,10 +630,6 @@
             pltpu.VMEM((4, 4, 4, ROWS, 4 * UNITS_PAD), jnp.float32),
             pltpu.VMEM((4, 4, 4, ROWS, HEAD_SIZE), jnp.float32),
             held(8, UNITS_PAD, MODEL),
-            held(CHUNKS, 3, 4, ROWS, size),
-            held(CHUNKS, 4, ROWS, size),
-            held(CHUNKS, 3, ROWS, size),
-            held(8, ROWS, MODEL),
             dma((7,)),
             dma((15,)),
             dma((15,)),
@@ -656,7 +654,7 @@
             dma((2, 7)),
         ],
         compiler_params=pltpu.CompilerParams(
-            collective_id=0, has_side_effects=True, vmem_limit_bytes=57 << 20
+            collective_id=0, has_side_effects=True, vmem_limit_bytes=51 << 20
         ),
         cost_estimate=pl.CostEstimate(flops=2 * 1024 * 5120 * 512, bytes_accessed=200 << 20, transcendentals=0),
     )(*operands)
@@ -695,7 +693,7 @@
         mid_parent,
         node_len,
         residual,
-        out_proj,
+        out_proj.reshape(QUERY_PER_KV * HEAD_SIZE // ROWS, ROWS, MODEL),
         norm_gain.reshape(1, -1),
         gate_proj.T,
         up_proj.T,

time: 130 us -> 126 us (0.969)
  local copies, waits for them, and re-layouts: 5.77 us -> 3.23 us
    unnamed x2 -> x28, local copies, waits for them, and re-layouts: 3.24 us -> 1.41 us
where the time goes in v5:
time: 126 us
  Pallas kernels  122 us (97%)
  local copies, waits for them, and re-layouts  3.23 us (3%)
    pallas_call x1, Pallas kernels, layer(): pl.pallas_call(layer_kernel, out_shape=(jax.ShapeDtypeStruct((ROWS, MODEL...  122 us

profile of v5, /device:TPU:1, one launch (start us, length us, event | category | flops | bytes accessed | tf_op | source)
XLA Modules:
  0.0 126.2 jit_solution(12576985535901176645)
XLA Ops:
  0.6 0.0 copy-start.8
  0.6 0.0 copy-start.5
  0.7 0.0 copy-start
  0.7 0.0 copy-start.4
  0.7 0.0 copy-start.12
  0.7 0.0 copy-start.11
  0.7 0.0 copy-start.10
  0.7 0.0 copy-start.9
  0.7 0.0 copy-start.7
  0.7 0.0 copy-start.6
  0.7 0.0 copy-start.3
  0.7 0.0 copy-start.2
  0.8 0.0 copy-start.1
  0.8 1.8 %reshape.19.pages_hbm = bf16[32,64,256]{2,1,0:T(8,128)(2,1)S(1)} reshape(bf16[32,64,2,128]{3,2,1,0:T(2,128)(2,1)} %param.22) | data formatting | bytes 2097152 | tf_op jit(solution)/shard_map/reshape | solution.py:688
  2.6 0.0 copy-done.8
  2.6 0.0 copy-done.5
  2.6 0.0 copy-done
  2.6 0.0 copy-done.4
  2.6 0.0 copy-done.12
  2.6 0.0 copy-done.11
  2.7 0.0 copy-done.10
  2.7 0.0 copy-done.9
  2.7 0.0 copy-done.7
  2.7 0.0 copy-done.6
  2.7 0.0 copy-done.3
  2.7 0.0 copy-done.2
  2.7 0.0 copy-done.1
  2.7 122.1 %shard_map.194 = (bf16[16,5120]{1,0:T(8,128)(2,1)S(1)}, bf16[128,896]{1,0:T(8,128)(2,1)S(1)}) custom-call(bf16[128,640]{1,0:T(8,128)(2,1)S(1)} %copy-done.1, bf16[128,128]{1,0:T(8,128)(2,1)S(1)} %copy-done.2, bf16[128,128]{1,0:T(8,128)(2,1)S(1)} %copy-done.3, bf16[32,64,256]{2,1,0:T(8,128)(2,1)S(1)} %reshape.19.pages_hbm, s32[6,4,16]{2,1,0:T(4,128)S(1)} %bitcast.11, ...), custom_call_target="tpu_custom_call" | custom-call | flops 5368709120 | bytes 209715200 | tf_op jit(solution)/shard_map/pallas_call | solution.py:600
  124.8 0.7 copy.23
  125.5 0.7 copy.24
Async XLA Ops:
  0.6 2.0 %copy-start.8 = (f32[896]{0:T(1024)S(1)}, f32[896]{0:T(1024)}, u32[]{:S(2)}) copy-start(f32[896]{0:T(1024)} %bias.1) | copy-start | bytes 10756
  0.6 2.0 %copy-start.5 = (f32[5120]{0:T(1024)S(1)}, f32[5120]{0:T(1024)}, u32[]{:S(2)}) copy-start(f32[5120]{0:T(1024)} %param.35) | copy-start | bytes 61444
  0.7 2.0 %copy-start = (bf16[5120,108]{0,1:T(8,128)(2,1)S(1)}, bf16[5120,108]{0,1:T(8,128)(2,1)}, u32[]{:S(2)}) copy-start(bf16[5120,108]{0,1:T(8,128)(2,1)} %param.32) | copy-start | bytes 3317764
  0.7 2.0 %copy-start.4 = (f32[5120]{0:T(1024)S(1)}, f32[5120]{0:T(1024)}, u32[]{:S(2)}) copy-start(f32[5120]{0:T(1024)} %param.31) | copy-start | bytes 61444
  0.7 2.0 %copy-start.12 = (s32[1,6]{1,0:T(1,128)S(1)}, s32[1,6]{1,0:T(1,128)}, u32[]{:S(2)}) copy-start(s32[1,6]{1,0:T(1,128)} %node_len.1) | copy-start | bytes 76
  0.7 2.0 %copy-start.11 = (s32[1,4]{1,0:T(1,128)S(1)}, s32[1,4]{1,0:T(1,128)}, u32[]{:S(2)}) copy-start(s32[1,4]{1,0:T(1,128)} %mid_parent.1) | copy-start | bytes 52
  0.7 2.0 %copy-start.10 = (s32[1,8]{1,0:T(1,128)S(1)}, s32[1,8]{1,0:T(1,128)}, u32[]{:S(2)}) copy-start(s32[1,8]{1,0:T(1,128)} %req_parent.1) | copy-start | bytes 100
  0.7 2.0 %copy-start.9 = (s32[128]{0:T(128)S(1)}, s32[128]{0:T(128)}, u32[]{:S(2)}) copy-start(s32[128]{0:T(128)} %param.25) | copy-start | bytes 1540
  0.7 2.0 %copy-start.7 = (s32[16,6,4]{0,2,1:T(4,128)S(1)}, s32[16,6,4]{0,2,1:T(4,128)}, u32[]{:S(2)}) copy-start(s32[16,6,4]{0,2,1:T(4,128)} %param.24) | copy-start | bytes 4612
  0.7 2.0 %copy-start.6 = (s32[16,6,4]{0,2,1:T(4,128)S(1)}, s32[16,6,4]{0,2,1:T(4,128)}, u32[]{:S(2)}) copy-start(s32[16,6,4]{0,2,1:T(4,128)} %param.23) | copy-start | bytes 4612
  0.7 2.0 %copy-start.3 = (bf16[128,128]{1,0:T(8,128)(2,1)S(1)}, bf16[128,128]{1,0:T(8,128)(2,1)}, u32[]{:S(2)}) copy-start(bf16[128,128]{1,0:T(8,128)(2,1)} %leaf_values.1) | copy-start | bytes 98308
  0.7 2.0 %copy-start.2 = (bf16[128,128]{1,0:T(8,128)(2,1)S(1)}, bf16[128,128]{1,0:T(8,128)(2,1)}, u32[]{:S(2)}) copy-start(bf16[128,128]{1,0:T(8,128)(2,1)} %leaf_keys.1) | copy-start | bytes 98308
  0.8 2.0 %copy-start.1 = (bf16[128,640]{1,0:T(8,128)(2,1)S(1)}, bf16[128,640]{1,0:T(8,128)(2,1)}, u32[]{:S(2)}) copy-start(bf16[128,640]{1,0:T(8,128)(2,1)} %queries.1) | copy-start | bytes 491524

commit v6 on v5

--- a/solution.py
+++ b/solution.py
@@ -27,7 +27,7 @@
 ENTRIES = 24
 PREFIX = NODES_DEV * NODE_MAX
 SLICES = 5
-CHUNKS = 4
+CHUNKS = 8
 HIDDEN = -1e30
 
 EPS = 1e-06

time: 126 us -> 126 us (level)
  no operation moved by 1% of the time
where the time goes in v6:
time: 126 us
  Pallas kernels  121 us (96%)
  local copies, waits for them, and re-layouts  3.23 us (3%)
    pallas_call x1, Pallas kernels, layer(): pl.pallas_call(layer_kernel, out_shape=(jax.ShapeDtypeStruct((ROWS, MODEL...  121 us

profile of v6, /device:TPU:1, one launch (start us, length us, event | category | flops | bytes accessed | tf_op | source)
XLA Modules:
  0.0 125.6 jit_solution(6092791940017215761)
XLA Ops:
  0.6 0.0 copy-start.8
  0.6 0.0 copy-start.5
  0.7 0.0 copy-start
  0.7 0.0 copy-start.4
  0.7 0.0 copy-start.12
  0.7 0.0 copy-start.11
  0.7 0.0 copy-start.10
  0.7 0.0 copy-start.9
  0.7 0.0 copy-start.7
  0.7 0.0 copy-start.6
  0.7 0.0 copy-start.3
  0.7 0.0 copy-start.2
  0.8 0.0 copy-start.1
  0.8 1.8 %reshape.19.pages_hbm = bf16[32,64,256]{2,1,0:T(8,128)(2,1)S(1)} reshape(bf16[32,64,2,128]{3,2,1,0:T(2,128)(2,1)} %param.22) | data formatting | bytes 2097152 | tf_op jit(solution)/shard_map/reshape | solution.py:688
  2.6 0.0 copy-done.8
  2.6 0.0 copy-done.5
  2.6 0.0 copy-done
  2.6 0.0 copy-done.4
  2.6 0.0 copy-done.12
  2.6 0.0 copy-done.11
  2.7 0.0 copy-done.10
  2.7 0.0 copy-done.9
  2.7 0.0 copy-done.7
  2.7 0.0 copy-done.6
  2.7 0.0 copy-done.3
  2.7 0.0 copy-done.2
  2.7 0.0 copy-done.1
  2.7 121.5 %shard_map.194 = (bf16[16,5120]{1,0:T(8,128)(2,1)S(1)}, bf16[128,896]{1,0:T(8,128)(2,1)S(1)}) custom-call(bf16[128,640]{1,0:T(8,128)(2,1)S(1)} %copy-done.1, bf16[128,128]{1,0:T(8,128)(2,1)S(1)} %copy-done.2, bf16[128,128]{1,0:T(8,128)(2,1)S(1)} %copy-done.3, bf16[32,64,256]{2,1,0:T(8,128)(2,1)S(1)} %reshape.19.pages_hbm, s32[6,4,16]{2,1,0:T(4,128)S(1)} %bitcast.11, ...), custom_call_target="tpu_custom_call" | custom-call | flops 5368709120 | bytes 209715200 | tf_op jit(solution)/shard_map/pallas_call | solution.py:600
  124.2 0.7 copy.23
  124.9 0.7 copy.24
Async XLA Ops:
  0.6 2.0 %copy-start.8 = (f32[896]{0:T(1024)S(1)}, f32[896]{0:T(1024)}, u32[]{:S(2)}) copy-start(f32[896]{0:T(1024)} %bias.1) | copy-start | bytes 10756
  0.6 2.0 %copy-start.5 = (f32[5120]{0:T(1024)S(1)}, f32[5120]{0:T(1024)}, u32[]{:S(2)}) copy-start(f32[5120]{0:T(1024)} %param.35) | copy-start | bytes 61444
  0.7 2.0 %copy-start = (bf16[5120,108]{0,1:T(8,128)(2,1)S(1)}, bf16[5120,108]{0,1:T(8,128)(2,1)}, u32[]{:S(2)}) copy-start(bf16[5120,108]{0,1:T(8,128)(2,1)} %param.32) | copy-start | bytes 3317764
  0.7 2.0 %copy-start.4 = (f32[5120]{0:T(1024)S(1)}, f32[5120]{0:T(1024)}, u32[]{:S(2)}) copy-start(f32[5120]{0:T(1024)} %param.31) | copy-start | bytes 61444
  0.7 2.0 %copy-start.12 = (s32[1,6]{1,0:T(1,128)S(1)}, s32[1,6]{1,0:T(1,128)}, u32[]{:S(2)}) copy-start(s32[1,6]{1,0:T(1,128)} %node_len.1) | copy-start | bytes 76
  0.7 2.0 %copy-start.11 = (s32[1,4]{1,0:T(1,128)S(1)}, s32[1,4]{1,0:T(1,128)}, u32[]{:S(2)}) copy-start(s32[1,4]{1,0:T(1,128)} %mid_parent.1) | copy-start | bytes 52
  0.7 2.0 %copy-start.10 = (s32[1,8]{1,0:T(1,128)S(1)}, s32[1,8]{1,0:T(1,128)}, u32[]{:S(2)}) copy-start(s32[1,8]{1,0:T(1,128)} %req_parent.1) | copy-start | bytes 100
  0.7 2.0 %copy-start.9 = (s32[128]{0:T(128)S(1)}, s32[128]{0:T(128)}, u32[]{:S(2)}) copy-start(s32[128]{0:T(128)} %param.25) | copy-start | bytes 1540
  0.7 2.0 %copy-start.7 = (s32[16,6,4]{0,2,1:T(4,128)S(1)}, s32[16,6,4]{0,2,1:T(4,128)}, u32[]{:S(2)}) copy-start(s32[16,6,4]{0,2,1:T(4,128)} %param.24) | copy-start | bytes 4612
  0.7 2.0 %copy-start.6 = (s32[16,6,4]{0,2,1:T(4,128)S(1)}, s32[16,6,4]{0,2,1:T(4,128)}, u32[]{:S(2)}) copy-start(s32[16,6,4]{0,2,1:T(4,128)} %param.23) | copy-start | bytes 4612
  0.7 2.0 %copy-start.3 = (bf16[128,128]{1,0:T(8,128)(2,1)S(1)}, bf16[128,128]{1,0:T(8,128)(2,1)}, u32[]{:S(2)}) copy-start(bf16[128,128]{1,0:T(8,128)(2,1)} %leaf_values.1) | copy-start | bytes 98308
  0.7 2.0 %copy-start.2 = (bf16[128,128]{1,0:T(8,128)(2,1)S(1)}, bf16[128,128]{1,0:T(8,128)(2,1)}, u32[]{:S(2)}) copy-start(bf16[128,128]{1,0:T(8,128)(2,1)} %leaf_keys.1) | copy-start | bytes 98308
  0.8 2.0 %copy-start.1 = (bf16[128,640]{1,0:T(8,128)(2,1)S(1)}, bf16[128,640]{1,0:T(8,128)(2,1)}, u32[]{:S(2)}) copy-start(bf16[128,640]{1,0:T(8,128)(2,1)} %queries.1) | copy-start | bytes 491524
